TPU v7x, 32 devices: a whole 2x2x4 slice. The times are simulated.
32 devices in a mesh: expert: 8 (over z, x), dp: 4 (over y, core).
Axes of the slice: x: 2, y: 2, z: 4, core: 2. Of those that a mesh axis runs over, the one named last changes fastest.
Arguments:
- enc_state: bfloat16 [4, 8, 256, 1024], P('dp', 'expert'), may hold values from -6 to 6
- baseline: bfloat16 [4, 8, 256, 1024], P('dp', 'expert'), may hold values from -6 to 6
- enc_keys: bfloat16 [4, 8, 256, 1024], P('dp', 'expert'), may hold values from -4 to 4
- dec_queries: bfloat16 [4, 8, 128, 1024], P('dp', 'expert'), may hold values from -200 to 200
- out_mult: bfloat16 [4, 8, 128, 1024], P('dp', 'expert'), may hold values from -6 to 6
- doc_lengths: int32 [4, 8], P('dp', 'expert'), may hold values from 128 to 256, as said below
- expert_ids: int32 [4, 8, 256], P('dp', 'expert'), may hold values from 0 to 15
- slot_ids: int32 [4, 8, 256], P('dp', 'expert'), may hold values from 0 to 31, as said below
- gate_prob: float32 [4, 8, 256], P('dp', 'expert'), may hold values from 0.2 to 1
- norm_gain: float32 [1024], replicated, may hold values from 0.5 to 2
- w_in: bfloat16 [16, 1024, 2816], P('expert', None, 'dp'), may hold values from -0.1875 to 0.1875
- w_out_t: bfloat16 [16, 1024, 2816], P('expert', None, 'dp'), may hold values from -0.109375 to 0.109375
- w_value: bfloat16 [1024, 1024], replicated, may hold values from -0.1875 to 0.1875
Outputs:
- enc_mult: bfloat16 [4, 8, 256, 1024], P('dp', 'expert')
Inputs may be any that keep to these rules, and one draw needn't show every extreme that they name: `slot_ids`: within one document no two tokens share an expert and a slot, and every token has a slot; one expert has all 32 slots used in every document. `doc_lengths`: some document has all 256 tokens.
All inputs are finite; a program needn't handle non-finite values.
Results may differ from a plain program's by a relative error of at most 0.0069.
Values may be sent and summed in bfloat16 or wider, within the bound.
A program may use at most 128 MiB of HBM per device.

v0:
```python
import math

import jax
import jax.numpy as jnp
from jax import lax
from jax.sharding import PartitionSpec as P

HEADS = 16
HEAD_DIM = 64


def rescale(pre_act, base_act):
    upper_part = jnp.maximum(jnp.maximum(pre_act, base_act), 0.0)
    lower_part = jnp.maximum(-jnp.minimum(pre_act, base_act), 0.0)
    return upper_part / (upper_part + lower_part + jnp.where(upper_part > 0.0, 0.0, 1.0))


def attend(query_rows, key_rows, mult_rows, length, w_value):
    enc_len = key_rows.shape[0]
    dec_len = query_rows.shape[0]
    queries = query_rows.reshape(dec_len, HEADS, HEAD_DIM)
    keys = key_rows.reshape(enc_len, HEADS, HEAD_DIM)
    mults = mult_rows.reshape(dec_len, HEADS, HEAD_DIM)
    scores = jnp.einsum("qhd,khd->hqk", queries, keys, preferred_element_type=jnp.float32) * (
        1.0 / math.sqrt(HEAD_DIM)
    )
    valid = jnp.arange(enc_len, dtype=jnp.int32) < length
    scores = jnp.where(valid[None, None, :], scores, -jnp.inf)
    top_score = jnp.max(scores, axis=-1, keepdims=True)
    expo = jnp.exp(scores - top_score)
    attn = (expo / jnp.sum(expo, axis=-1, keepdims=True)).astype(jnp.bfloat16)
    value_mult = jnp.einsum("hqk,qhd->khd", attn, mults, preferred_element_type=jnp.float32).astype(
        jnp.bfloat16
    )
    return lax.dot_general(
        value_mult.reshape(enc_len, HEADS * HEAD_DIM),
        w_value,
        (((1,), (1,)), ((), ())),
        preferred_element_type=jnp.float32,
    )


def expert_terms(rows_in, rows_base, rows_mult, part_in, part_out):
    pre_act = jnp.einsum("erd,edf->erf", rows_in, part_in, preferred_element_type=jnp.float32)
    base_act = jnp.einsum("erd,edf->erf", rows_base, part_in, preferred_element_type=jnp.float32)
    hidden_mult = jnp.einsum(
        "erd,edf->erf", rows_mult, part_out, preferred_element_type=jnp.float32
    )
    act_mult = (rescale(pre_act, base_act) * hidden_mult).astype(jnp.bfloat16)
    return jnp.einsum("erf,edf->erd", act_mult, part_in, preferred_element_type=jnp.float32)


def body(
    enc_state,
    baseline,
    enc_keys,
    dec_queries,
    out_mult,
    doc_lengths,
    expert_ids,
    slot_ids,
    gate_prob,
    norm_gain,
    w_in,
    w_out_t,
    w_value,
):
    enc_len = enc_state.shape[2]
    feature_width = enc_state.shape[3]
    local_experts = w_in.shape[0]
    n_experts = local_experts * lax.axis_size("expert")
    capacity = max(2, 2 * enc_len // n_experts)
    tokens = enc_state[0, 0].astype(jnp.float32)
    row_scale = norm_gain * lax.rsqrt(jnp.mean(tokens * tokens, axis=-1, keepdims=True) + 1e-06)
    inputs = (tokens * row_scale).astype(jnp.bfloat16)
    base_inputs = (baseline[0, 0].astype(jnp.float32) * row_scale).astype(jnp.bfloat16)
    flat_slot = expert_ids[0, 0] * capacity + slot_ids[0, 0]
    onehot = (
        flat_slot[None, :] == jnp.arange(n_experts * capacity, dtype=jnp.int32)[:, None]
    ).astype(jnp.bfloat16)

    def dispatch(values):
        placed = jnp.dot(onehot, values, preferred_element_type=jnp.float32).astype(jnp.bfloat16)
        return placed.reshape(n_experts, capacity, feature_width)

    layer_mult = attend(
        dec_queries[0, 0], enc_keys[0, 0], out_mult[0, 0], doc_lengths[0, 0], w_value
    )
    scaled_mult = (gate_prob[0, 0][:, None] * layer_mult).astype(jnp.bfloat16)
    sent_in, sent_base, sent_mult = (
        lax.all_to_all(dispatch(inputs), "expert", split_axis=0, concat_axis=1, tiled=True),
        lax.all_to_all(dispatch(base_inputs), "expert", split_axis=0, concat_axis=1, tiled=True),
        lax.all_to_all(dispatch(scaled_mult), "expert", split_axis=0, concat_axis=1, tiled=True),
    )
    slot_mult = expert_terms(
        sent_in,
        sent_base,
        sent_mult,
        lax.all_gather(w_in, "dp", axis=2, tiled=True),
        lax.all_gather(w_out_t, "dp", axis=2, tiled=True),
    )
    returned = lax.all_to_all(
        slot_mult.astype(jnp.bfloat16), "expert", split_axis=1, concat_axis=0, tiled=True
    )
    per_token = lax.dot_general(
        onehot,
        returned.reshape(n_experts * capacity, feature_width),
        (((0,), (0,)), ((), ())),
        preferred_element_type=jnp.float32,
    )
    result = (layer_mult + row_scale * per_token).astype(jnp.bfloat16)
    return result[None, None]


def solution(mesh):
    in_specs = (
        P("dp", "expert", None, None),
        P("dp", "expert", None, None),
        P("dp", "expert", None, None),
        P("dp", "expert", None, None),
        P("dp", "expert", None, None),
        P("dp", "expert"),
        P("dp", "expert", None),
        P("dp", "expert", None),
        P("dp", "expert", None),
        P(),
        P("expert", None, "dp"),
        P("expert", None, "dp"),
        P(),
    )
    out_specs = P("dp", "expert", None, None)
    return jax.shard_map(body, mesh=mesh, in_specs=in_specs, out_specs=out_specs, check_vma=False)
```

profile of v0, /device:TPU:0, one launch (start us, length us, event | category | flops | bytes accessed | tf_op | source)
XLA Modules:
  0.0 230.6 jit_solution(66276424766294604)
XLA Ops:
  6.5 0.0 copy-start
  6.5 0.0 copy-start.4
  6.5 0.0 copy-start.8
  6.5 0.0 copy-start.9
  6.5 0.0 copy-start.6
  6.5 0.0 all-gather.3.cloned.1.call-start
  6.6 0.7 all-gather.3.cloned.1.call-update
  7.3 0.0 copy-start.5
  7.3 0.0 all-gather.5.cloned.1.call-start
  7.3 0.7 all-gather.5.cloned.1.call-update
  8.0 0.0 copy-done.4
  8.1 0.2 fusion.5
  8.2 0.0 copy-done.8
  8.3 0.0 copy-done.9
  8.3 0.0 copy-done.6
  8.3 2.6 %convolution_convert_fusion.1 = bf16[512,1024]{1,0:T(8,128)(2,1)} fusion(bf16[1,1,256,1024]{3,2,1,0:T(8,128)(2,1)} %param.14, f32[256]{0:T(256)S(1)} %add_rsqrt_fusion, f32[1024]{0:T(1024)S(1)} %copy-done.6, s32[256]{0:T(256)S(1)} %bitcast.71), kind=kOutput, calls=%fused_computation.10 | convolution fusion | flops 270139392 | bytes 1579008 | tf_op jit(solution)/shard_map/dot_general | solution.py:83
  10.9 7.3 %all-to-all-start.1 = ((bf16[16,32,1024]{2,1,0:T(8,128)(2,1)}), bf16[16,32,1024]{2,1,0:T(8,128)(2,1)S(1)}, u32[]{:S(2)}, u32[]{:S(2)}) async-start(bf16[16,32,1024]{2,1,0:T(8,128)(2,1)} %bitcast.66), calls=%async_computation.1 | async-start | bytes 2097152 | tf_op jit(solution)/shard_map/all_to_all | solution.py:92
  18.2 2.6 %convolution_convert_fusion.2 = bf16[512,1024]{1,0:T(8,128)(2,1)} fusion(bf16[1,1,256,1024]{3,2,1,0:T(8,128)(2,1)} %param.13, f32[256]{0:T(256)S(1)} %add_rsqrt_fusion, f32[1024]{0:T(1024)S(1)} %copy-done.6, s32[256]{0:T(256)S(1)} %bitcast.72), kind=kOutput, calls=%fused_computation.11 | convolution fusion | flops 270139392 | bytes 1579008 | tf_op jit(solution)/shard_map/dot_general | solution.py:83
  20.8 23.1 %all-to-all-done.1 = bf16[16,32,1024]{2,1,0:T(8,128)(2,1)S(1)} async-done(((bf16[16,32,1024]{2,1,0:T(8,128)(2,1)}), bf16[16,32,1024]{2,1,0:T(8,128)(2,1)S(1)}, u32[]{:S(2)}, u32[]{:S(2)}) %all-to-all-start.1) | async-done | bytes 1048608 | tf_op jit(solution)/shard_map/all_to_all | solution.py:92
  44.0 0.0 copy-start.2
  44.0 4.2 %all-to-all-start = ((bf16[16,32,1024]{2,1,0:T(8,128)(2,1)}), bf16[16,32,1024]{2,1,0:T(8,128)(2,1)}, u32[]{:S(2)}, u32[]{:S(2)}) async-start(bf16[16,32,1024]{2,1,0:T(8,128)(2,1)} %bitcast.62), calls=%async_computation | async-start | bytes 2097152 | tf_op jit(solution)/shard_map/all_to_all | solution.py:91
  48.9 0.0 copy-done.5
  48.9 0.8 copy.39
  49.7 1.1 copy.41
  50.8 2.0 copy.40
  52.9 3.2 %fusion.28 = (f32[16,128]{1,0:T(8,128)S(1)}, f32[16,128,256]{2,1,0:T(8,128)}) fusion(pred[256]{0:T(512)(128)(4,1)S(1)} %iota_compare_fusion.5, bf16[128,16,64]{0,2,1:T(8,128)(2,1)} %bitcast.70, bf16[256,16,64]{0,2,1:T(8,128)(2,1)} %bitcast.68), kind=kOutput, calls=%fused_computation.43 | convolution fusion | flops 69206272 | bytes 2892032 | tf_op jit(solution)/shard_map/sub | solution.py:30
  56.0 0.0 copy-start.7
  56.0 2.2 convolution_convert_fusion.4
  58.2 0.0 copy-done.2
  58.3 0.0 copy-done
  58.3 0.8 fusion.29
  59.0 0.0 copy-done.7
  59.1 1.5 convolution_convert_fusion
  60.6 13.2 %all-to-all-done = bf16[16,32,1024]{2,1,0:T(8,128)(2,1)} async-done(((bf16[16,32,1024]{2,1,0:T(8,128)(2,1)}), bf16[16,32,1024]{2,1,0:T(8,128)(2,1)}, u32[]{:S(2)}, u32[]{:S(2)}) %all-to-all-start) | async-done | bytes 1048608 | tf_op jit(solution)/shard_map/all_to_all | solution.py:91
  73.8 3.7 %all-to-all-start.2 = ((bf16[16,32,1024]{2,1,0:T(8,128)(2,1)}), bf16[16,32,1024]{2,1,0:T(8,128)(2,1)S(1)}, u32[]{:S(2)}, u32[]{:S(2)}) async-start(bf16[16,32,1024]{2,1,0:T(8,128)(2,1)} %bitcast.19), calls=%async_computation.2 | async-start | bytes 2097152 | tf_op jit(solution)/shard_map/all_to_all | solution.py:93
  77.5 1.3 copy.43
  78.8 2.4 %copy.42 = bf16[8,2,32,1024]{3,2,0,1:T(8,128)(2,1)} copy(bf16[8,2,32,1024]{3,2,1,0:T(8,128)(2,1)} %bitcast.10) | data formatting | bytes 2097152 | tf_op jit(solution)/shard_map/all_to_all | solution.py:91
  81.3 22.0 %all-to-all-done.2 = bf16[16,32,1024]{2,1,0:T(8,128)(2,1)S(1)} async-done(((bf16[16,32,1024]{2,1,0:T(8,128)(2,1)}), bf16[16,32,1024]{2,1,0:T(8,128)(2,1)S(1)}, u32[]{:S(2)}, u32[]{:S(2)}) %all-to-all-start.2) | async-done | bytes 1048608 | tf_op jit(solution)/shard_map/all_to_all | solution.py:93
  103.2 1.1 copy.44
  104.3 0.0 all-gather.3.cloned.1.call-done
  104.3 10.3 %fusion.30 = f32[2,256,2816]{2,1,0:T(8,128)} fusion(bf16[2,256,1024]{2,1,0:T(8,128)(2,1)} %bitcast.65, bf16[2,1024,2816]{1,2,0:T(8,128)(2,1)} %all-gather.3.cloned.1.call-done), kind=kOutput, calls=%fused_computation.45 | convolution fusion | flops 2952790016 | bytes 18350080 | tf_op jit(solution)/shard_map/erd,edf->erf/dot_general | solution.py:44
  114.6 0.0 copy-start.3
  114.6 13.8 %fusion.31 = f32[2,256,2816]{2,1,0:T(8,128)} fusion(bf16[2,256,1024]{2,1,0:T(8,128)(2,1)S(1)} %bitcast.63, bf16[2,1024,2816]{1,2,0:T(8,128)(2,1)} %all-gather.3.cloned.1.call-done), kind=kOutput, calls=%fused_computation.46 | convolution fusion | flops 2952790016 | bytes 18350080 | tf_op jit(solution)/shard_map/erd,edf->erf/dot_general | solution.py:45
  128.4 37.1 %all-gather.5.cloned.1.call-done = bf16[2,1024,2816]{1,2,0:T(8,128)(2,1)} async-done(((bf16[2,1024,704]{1,2,0:T(8,128)(2,1)}), bf16[2,1024,2816]{1,2,0:T(8,128)(2,1)}) %all-gather.5.cloned.1.call-update) | async-done | bytes 11534352 | tf_op jit(solution)/shard_map/all_gather | solution.py:100
  165.5 0.0 copy-done.3
  165.5 15.6 %multiply_convert_fusion = bf16[2,256,2816]{2,1,0:T(8,128)(2,1)} fusion(f32[2,256,2816]{2,1,0:T(8,128)} %fusion.30, f32[2,256,2816]{2,1,0:T(8,128)} %fusion.31, bf16[2,256,1024]{2,1,0:T(8,128)(2,1)S(1)} %bitcast.64, bf16[2,1024,2816]{1,2,0:T(8,128)(2,1)} %all-gather.5.cloned.1.call-done), kind=kOutput, calls=%fused_computation.1 | convolution fusion | flops 2970091520 | bytes 27000832 | tf_op jit(solution)/shard_map/erd,edf->erf/dot_general | solution.py:46
  181.1 0.0 copy-start.1
  181.1 8.4 %convolution_convert_fusion.3 = bf16[2,256,1024]{2,1,0:T(8,128)(2,1)S(1)} fusion(bf16[2,256,2816]{2,1,0:T(8,128)(2,1)} %multiply_convert_fusion, bf16[2,1024,2816]{1,2,0:T(8,128)(2,1)} %all-gather.3.cloned.1.call-done), kind=kOutput, calls=%fused_computation.12 | convolution fusion | flops 2953314304 | bytes 15466496 | tf_op jit(solution)/shard_map/erf,edf->erd/dot_general | solution.py:50
  189.5 1.1 copy.45
  190.6 31.4 %all_to_all.69 = bf16[2,256,1024]{2,0,1:T(2,128)(2,1)S(1)} all-to-all(bf16[2,256,1024]{2,0,1:T(2,128)(2,1)S(1)} %copy.45), channel_id=1, replica_groups=mesh['expert'=8,'dp'=4] {'expert'}, dimensions={1} | all-to-all | bytes 2097152 | tf_op jit(solution)/shard_map/all_to_all | solution.py:102
  222.1 0.3 copy.46
  222.3 0.1 copy.47
  222.4 1.3 fusion.4
  223.7 0.0 copy-done.1
  (3 shorter events, 0.0 us)
Async XLA Ops:
  6.5 51.7 %copy-start = (bf16[1024,1024]{1,0:T(8,128)(2,1)S(1)}, bf16[1024,1024]{1,0:T(8,128)(2,1)}, u32[]{:S(2)}) copy-start(bf16[1024,1024]{1,0:T(8,128)(2,1)} %param.25) | copy-start | bytes 6291460
  6.5 1.5 copy-start.4
  6.5 1.7 copy-start.8
  6.5 1.7 copy-start.9
  6.5 1.7 copy-start.6
  6.5 97.8 %all-gather.3.cloned.1.call-start = ((), (), s32[]{:S(2)}) async-start(), calls=%async_computation.4 | async-start | bytes 14417920 | tf_op jit(solution)/shard_map/all_gather | solution.py:99
  7.3 41.6 %copy-start.5 = (bf16[1,1,128,1024]{3,2,1,0:T(8,128)(2,1)S(1)}, bf16[1,1,128,1024]{3,2,1,0:T(8,128)(2,1)}, u32[]{:S(2)}) copy-start(bf16[1,1,128,1024]{3,2,1,0:T(8,128)(2,1)} %param.16) | copy-start | bytes 786436
  7.3 158.2 %all-gather.5.cloned.1.call-start = ((), (), s32[]{:S(2)}) async-start(), calls=%async_computation.5 | async-start | bytes 14417920 | tf_op jit(solution)/shard_map/all_gather | solution.py:100
  10.9 33.0 %all-to-all-start.1 = ((bf16[16,32,1024]{2,1,0:T(8,128)(2,1)}), bf16[16,32,1024]{2,1,0:T(8,128)(2,1)S(1)}, u32[]{:S(2)}, u32[]{:S(2)}) async-start(bf16[16,32,1024]{2,1,0:T(8,128)(2,1)} %bitcast.66), calls=%async_computation.1 | async-start | bytes 2097152 | tf_op jit(solution)/shard_map/all_to_all | solution.py:92
  44.0 14.3 %copy-start.2 = (bf16[16,32,1024]{2,1,0:T(8,128)(2,1)}, bf16[16,32,1024]{2,1,0:T(8,128)(2,1)S(1)}, u32[]{:S(2)}) copy-start(bf16[16,32,1024]{2,1,0:T(8,128)(2,1)S(1)} %all-to-all-done.1) | copy-start | bytes 3145732
  44.0 29.8 %all-to-all-start = ((bf16[16,32,1024]{2,1,0:T(8,128)(2,1)}), bf16[16,32,1024]{2,1,0:T(8,128)(2,1)}, u32[]{:S(2)}, u32[]{:S(2)}) async-start(bf16[16,32,1024]{2,1,0:T(8,128)(2,1)} %bitcast.62), calls=%async_computation | async-start | bytes 2097152 | tf_op jit(solution)/shard_map/all_to_all | solution.py:91
  56.0 3.0 %copy-start.7 = (f32[1,1,256]{2,1,0:T(1,128)S(1)}, f32[1,1,256]{2,1,0:T(1,128)}, u32[]{:S(2)}) copy-start(f32[1,1,256]{2,1,0:T(1,128)} %param.21) | copy-start | bytes 3076
  73.8 29.5 %all-to-all-start.2 = ((bf16[16,32,1024]{2,1,0:T(8,128)(2,1)}), bf16[16,32,1024]{2,1,0:T(8,128)(2,1)S(1)}, u32[]{:S(2)}, u32[]{:S(2)}) async-start(bf16[16,32,1024]{2,1,0:T(8,128)(2,1)} %bitcast.19), calls=%async_computation.2 | async-start | bytes 2097152 | tf_op jit(solution)/shard_map/all_to_all | solution.py:93
  114.6 50.9 %copy-start.3 = (bf16[2,8,32,1024]{3,2,1,0:T(8,128)(2,1)S(1)}, bf16[2,8,32,1024]{3,2,1,0:T(8,128)(2,1)}, u32[]{:S(2)}) copy-start(bf16[2,8,32,1024]{3,2,1,0:T(8,128)(2,1)} %copy.44) | copy-start | bytes 3145732
  181.1 42.6 %copy-start.1 = (bf16[1024,1024]{1,0:T(8,128)(2,1)S(1)}, bf16[1024,1024]{1,0:T(8,128)(2,1)}, u32[]{:S(2)}) copy-start(bf16[1024,1024]{1,0:T(8,128)(2,1)} %param.25) | copy-start | bytes 6291460
Sparse Core Ops, SparseCore 0:
  8.9 78.8 all-gather.2
  89.4 76.1 all-gather.4
where the time goes:
time: 231 us
  waiting for transfers between devices  96.8 us (42%)
  matrix products  62.3 us (27%)
  blocking collectives  31.4 us (14%)
  starting transfers between devices  15.3 us (7%)
  between operations  14.2 us (6%)
  local copies, waits for them, and re-layouts  10.3 us (4%)
    all_gather x1, waiting for transfers between devices, body(): lax.all_gather(w_out_t, 'dp', axis=2, tiled=True)  37.1 us
    all_to_all x1, blocking collectives, body(): lax.all_to_all(slot_mult.astype(jnp.bfloat16), 'expert', split_axis=1, co...  31.4 us
    all_to_all x1, waiting for transfers between devices, body(): lax.all_to_all(dispatch(base_inputs), 'expert', split_axis=0, concat_axis...  23.1 us
    all_to_all x1, waiting for transfers between devices, body(): lax.all_to_all(dispatch(scaled_mult), 'expert', split_axis=0, concat_axis...  22 us
    dot_general x1, matrix products, expert_terms(): jnp.einsum('erd,edf->erf', rows_mult, part_out, preferred_element_type=jn...  15.6 us
    dot_general x1, matrix products, expert_terms(): jnp.einsum('erd,edf->erf', rows_base, part_in, preferred_element_type=jnp...  13.8 us
    all_to_all x1, waiting for transfers between devices, body(): lax.all_to_all(dispatch(inputs), 'expert', split_axis=0, concat_axis=1, t...  13.2 us
    dot_general x1, matrix products, expert_terms(): jnp.einsum('erd,edf->erf', rows_in, part_in, preferred_element_type=jnp.f...  10.3 us
  transfers between devices with their start and end apart: 5, of which 4 were waited for; matrix products, arithmetic and copies ran while one was open for 20% of the time, Pallas kernels for 0%

commit v1 on v0

--- a/solution.py
+++ b/solution.py
@@ -69,7 +69,15 @@
     feature_width = enc_state.shape[3]
     local_experts = w_in.shape[0]
     n_experts = local_experts * lax.axis_size("expert")
+    n_dp = lax.axis_size("dp")
+    near = 2 if n_dp % 2 == 0 else 1
     capacity = max(2, 2 * enc_len // n_experts)
+
+    shards = [(w_in, w_out_t)]
+    if near == 2:
+        swap = [(i, i ^ 1) for i in range(n_dp)]
+        shards.append((lax.ppermute(w_in, "dp", swap), lax.ppermute(w_out_t, "dp", swap)))
+
     tokens = enc_state[0, 0].astype(jnp.float32)
     row_scale = norm_gain * lax.rsqrt(jnp.mean(tokens * tokens, axis=-1, keepdims=True) + 1e-06)
     inputs = (tokens * row_scale).astype(jnp.bfloat16)
@@ -81,24 +89,35 @@
 
     def dispatch(values):
         placed = jnp.dot(onehot, values, preferred_element_type=jnp.float32).astype(jnp.bfloat16)
-        return placed.reshape(n_experts, capacity, feature_width)
+        placed = placed.reshape(n_experts, capacity, feature_width)
+        return lax.all_to_all(placed, "expert", split_axis=0, concat_axis=1, tiled=True)
 
+    sent_in = dispatch(inputs)
+    sent_base = dispatch(base_inputs)
     layer_mult = attend(
         dec_queries[0, 0], enc_keys[0, 0], out_mult[0, 0], doc_lengths[0, 0], w_value
     )
     scaled_mult = (gate_prob[0, 0][:, None] * layer_mult).astype(jnp.bfloat16)
-    sent_in, sent_base, sent_mult = (
-        lax.all_to_all(dispatch(inputs), "expert", split_axis=0, concat_axis=1, tiled=True),
-        lax.all_to_all(dispatch(base_inputs), "expert", split_axis=0, concat_axis=1, tiled=True),
-        lax.all_to_all(dispatch(scaled_mult), "expert", split_axis=0, concat_axis=1, tiled=True),
-    )
-    slot_mult = expert_terms(
-        sent_in,
-        sent_base,
-        sent_mult,
-        lax.all_gather(w_in, "dp", axis=2, tiled=True),
-        lax.all_gather(w_out_t, "dp", axis=2, tiled=True),
-    )
+    sent_mult = dispatch(scaled_mult)
+    own_rows = (sent_in, sent_base, sent_mult)
+
+    def partial_sum(rows):
+        total = expert_terms(*rows, *shards[0])
+        for part in shards[1:]:
+            total = total + expert_terms(*rows, *part)
+        return total
+
+    far = n_dp // near
+    far_rows = []
+    for hop in range(1, far):
+        ahead = [(i, (i + hop * near) % n_dp) for i in range(n_dp)]
+        far_rows.append(tuple(lax.ppermute(a, "dp", ahead) for a in own_rows))
+    slot_mult = partial_sum(own_rows)
+    for hop in range(1, far):
+        back = [((i + hop * near) % n_dp, i) for i in range(n_dp)]
+        far_part = partial_sum(far_rows[hop - 1]).astype(jnp.bfloat16)
+        slot_mult = slot_mult + lax.ppermute(far_part, "dp", back).astype(jnp.float32)
+
     returned = lax.all_to_all(
         slot_mult.astype(jnp.bfloat16), "expert", split_axis=1, concat_axis=0, tiled=True
     )

time: 231 us -> 235 us (1.017)
  between operations: 14.2 us -> 0.85 us
  matrix products: 62.3 us -> 73.8 us
  starting transfers between devices: 15.3 us -> 21.6 us
  waiting for transfers between devices: 96.8 us -> 92.1 us
  other arithmetic: 0.2 us -> 4.38 us
    all_gather x2 -> x0, waiting for transfers between devices: 37.1 us -> none  [the longest x1 37.1 us: body(): lax.all_gather(w_out_t, 'dp', axis=2, tiled=True)]
    ppermute x0 -> x6, waiting for transfers between devices: none -> 29 us  [the longest x3 17.5 us: body(): far_rows.append(tuple((lax.ppermute(a, 'dp', ahead) for a in own_rows)))]
    dot_general x1 -> x4, matrix products: 8.43 us -> 29.8 us  [expert_terms(): jnp.einsum('erf,edf->erd', act_mult, part_in, preferred_element_type=jnp....]
    dot_general x1 -> x0, matrix products: 15.6 us -> none  [expert_terms(): jnp.einsum('erd,edf->erf', rows_mult, part_out, preferred_element_type=jn...]
    dot_general x1 -> x4, matrix products: 10.3 us -> 16.1 us  [expert_terms(): jnp.einsum('erd,edf->erf', rows_in, part_in, preferred_element_type=jnp.f...]
    ppermute x0 -> x6, starting transfers between devices: none -> 5.64 us  [the longest x3 3.55 us: body(): far_rows.append(tuple((lax.ppermute(a, 'dp', ahead) for a in own_rows)))]
    all_to_all x3, waiting for transfers between devices: 58.3 us -> 63.1 us  [dispatch(): lax.all_to_all(placed, 'expert', split_axis=0, concat_axis=1, tiled=True)]
    convert_element_type x0 -> x1, other arithmetic: none -> 3.14 us  [body(): slot_mult.astype(jnp.bfloat16)]
  transfers between devices with their start and end apart: 5 -> 9, of which waited for: 4 -> 6; matrix products, arithmetic and copies ran while one was open for 20% -> 28% of each run, Pallas kernels for 0% -> 0%
where the time goes in v1:
time: 235 us; the launch traced here: 234 us
  waiting for transfers between devices  92.1 us (39%)
  matrix products  73.8 us (31%)
  blocking collectives  29.5 us (13%)
  starting transfers between devices  21.6 us (9%)
  local copies, waits for them, and re-layouts  12 us (5%)
  other arithmetic  4.38 us (2%)
    all_to_all x3, waiting for transfers between devices, dispatch(): lax.all_to_all(placed, 'expert', split_axis=0, concat_axis=1, tiled=True)  63.1 us
    dot_general x4, matrix products, expert_terms(): jnp.einsum('erf,edf->erd', act_mult, part_in, preferred_element_type=jnp....  29.8 us
    all_to_all x1, blocking collectives, body(): lax.all_to_all(slot_mult.astype(jnp.bfloat16), 'expert', split_axis=1, co...  29.5 us
    ppermute x3, waiting for transfers between devices, body(): far_rows.append(tuple((lax.ppermute(a, 'dp', ahead) for a in own_rows)))  17.5 us
    dot_general x4, matrix products, expert_terms(): jnp.einsum('erd,edf->erf', rows_in, part_in, preferred_element_type=jnp.f...  16.1 us
    all_to_all x3, starting transfers between devices, dispatch(): lax.all_to_all(placed, 'expert', split_axis=0, concat_axis=1, tiled=True)  15.9 us
    dot_general x4, matrix products, expert_terms(): jnp.einsum('erd,edf->erf', rows_base, part_in, preferred_element_type=jnp...  15 us
    ppermute x1, waiting for transfers between devices, body(): lax.ppermute(far_part, 'dp', back).astype(jnp.float32)  11.5 us
  transfers between devices with their start and end apart: 9, of which 6 were waited for; matrix products, arithmetic and copies ran while one was open for 28% of the time, Pallas kernels for 0%

profile of v1, /device:TPU:0, one launch (start us, length us, event | category | flops | bytes accessed | tf_op | source)
XLA Modules:
  0.0 234.2 jit_solution(12042869311677658196)
XLA Ops:
  0.0 0.0 copy-start
  0.0 1.4 copy.40
  1.4 1.1 copy.39
  3.2 1.1 copy.41
  4.3 2.0 fusion.48
  6.3 2.1 convolution_convert_fusion.3
  8.5 0.0 copy-start.5
  8.5 0.0 copy-start.6
  8.5 0.0 copy-start.4
  8.5 0.0 copy-done
  8.5 0.8 fusion.55
  9.3 0.0 copy-done.5
  9.3 0.0 copy-done.6
  9.4 0.0 copy-done.4
  9.4 0.0 copy-start.3
  9.4 1.5 convolution_convert_fusion
  10.9 7.3 %all-to-all-start.2 = ((bf16[16,32,1024]{2,1,0:T(8,128)(2,1)}), bf16[16,32,1024]{2,1,0:T(8,128)(2,1)}, u32[]{:S(2)}, u32[]{:S(2)}) async-start(bf16[16,32,1024]{2,1,0:T(8,128)(2,1)} %bitcast.78), calls=%async_computation.2 | async-start | bytes 2097152 | tf_op jit(solution)/shard_map/all_to_all | solution.py:93
  18.1 1.2 fusion.7
  19.4 0.0 copy-done.3
  19.4 2.6 %convolution_convert_fusion.2 = bf16[512,1024]{1,0:T(8,128)(2,1)} fusion(bf16[1,1,256,1024]{3,2,1,0:T(8,128)(2,1)} %param.13, f32[256]{0:T(256)S(1)} %add_rsqrt_fusion, f32[1024]{0:T(1024)S(1)} %copy-done.3, s32[256]{0:T(256)S(1)} %bitcast.88), kind=kOutput, calls=%fused_computation.12 | convolution fusion | flops 270139392 | bytes 1579008 | tf_op jit(solution)/shard_map/dot_general | solution.py:91
  22.0 22.0 %all-to-all-done.2 = bf16[16,32,1024]{2,1,0:T(8,128)(2,1)} async-done(((bf16[16,32,1024]{2,1,0:T(8,128)(2,1)}), bf16[16,32,1024]{2,1,0:T(8,128)(2,1)}, u32[]{:S(2)}, u32[]{:S(2)}) %all-to-all-start.2) | async-done | bytes 1048608 | tf_op jit(solution)/shard_map/all_to_all | solution.py:93
  44.0 4.2 %all-to-all-start = ((bf16[16,32,1024]{2,1,0:T(8,128)(2,1)}), bf16[16,32,1024]{2,1,0:T(8,128)(2,1)}, u32[]{:S(2)}, u32[]{:S(2)}) async-start(bf16[16,32,1024]{2,1,0:T(8,128)(2,1)} %bitcast.82), calls=%async_computation | async-start | bytes 2097152 | tf_op jit(solution)/shard_map/all_to_all | solution.py:93
  48.3 2.6 %convolution_convert_fusion.1 = bf16[512,1024]{1,0:T(8,128)(2,1)} fusion(bf16[1,1,256,1024]{3,2,1,0:T(8,128)(2,1)} %param.14, f32[256]{0:T(256)S(1)} %add_rsqrt_fusion, f32[1024]{0:T(1024)S(1)} %copy-done.3, s32[256]{0:T(256)S(1)} %bitcast.89), kind=kOutput, calls=%fused_computation.11 | convolution fusion | flops 270139392 | bytes 1579008 | tf_op jit(solution)/shard_map/dot_general | solution.py:91
  50.8 23.0 %all-to-all-done = bf16[16,32,1024]{2,1,0:T(8,128)(2,1)} async-done(((bf16[16,32,1024]{2,1,0:T(8,128)(2,1)}), bf16[16,32,1024]{2,1,0:T(8,128)(2,1)}, u32[]{:S(2)}, u32[]{:S(2)}) %all-to-all-start) | async-done | bytes 1048608 | tf_op jit(solution)/shard_map/all_to_all | solution.py:93
  73.8 4.4 %all-to-all-start.1 = ((bf16[16,32,1024]{2,1,0:T(8,128)(2,1)}), bf16[16,32,1024]{2,1,0:T(8,128)(2,1)}, u32[]{:S(2)}, u32[]{:S(2)}) async-start(bf16[16,32,1024]{2,1,0:T(8,128)(2,1)} %bitcast.81), calls=%async_computation.1 | async-start | bytes 2097152 | tf_op jit(solution)/shard_map/all_to_all | solution.py:93
  78.3 0.1 collective-permute-start
  78.4 0.5 collective-permute-start.1
  78.8 2.3 copy.44
  81.1 1.5 collective-permute-start.4
  82.7 2.3 copy.42
  85.0 0.5 collective-permute-start.2
  85.5 18.1 %all-to-all-done.1 = bf16[16,32,1024]{2,1,0:T(8,128)(2,1)} async-done(((bf16[16,32,1024]{2,1,0:T(8,128)(2,1)}), bf16[16,32,1024]{2,1,0:T(8,128)(2,1)}, u32[]{:S(2)}, u32[]{:S(2)}) %all-to-all-start.1) | async-done | bytes 1048608 | tf_op jit(solution)/shard_map/all_to_all | solution.py:93
  103.5 2.3 copy.43
  105.8 0.0 copy-start.1
  105.8 1.5 collective-permute-start.3
  107.3 4.3 %fusion.56 = f32[2,256,704]{1,2,0:T(8,128)} fusion(bf16[2,256,1024]{2,1,0:T(8,128)(2,1)} %bitcast.12, bf16[2,1024,704]{1,2,0:T(8,128)(2,1)} %param.23), kind=kOutput, calls=%fused_computation.72 | convolution fusion | flops 738197504 | bytes 5373952 | tf_op jit(solution)/shard_map/erd,edf->erf/dot_general | solution.py:44
  111.6 0.0 copy-done.1
  111.6 3.3 %fusion.57 = f32[2,256,704]{1,2,0:T(8,128)} fusion(bf16[2,256,1024]{2,1,0:T(8,128)(2,1)} %bitcast.17, bf16[2,1024,704]{1,2,0:T(8,128)(2,1)S(1)} %copy-done.1), kind=kOutput, calls=%fused_computation.73 | convolution fusion | flops 738197504 | bytes 5373952 | tf_op jit(solution)/shard_map/erd,edf->erf/dot_general | solution.py:45
  114.9 7.3 %fusion.6 = f32[2,256,1024]{2,1,0:T(8,128)} fusion(bf16[2,1024,704]{1,2,0:T(8,128)(2,1)} %param.23, bf16[2,256,1024]{2,1,0:T(8,128)(2,1)} %bitcast.22, bf16[2,1024,704]{1,2,0:T(8,128)(2,1)} %param.24, f32[2,256,704]{1,2,0:T(8,128)} %fusion.56, f32[2,256,704]{1,2,0:T(8,128)} %fusion.57), kind=kOutput, calls=%fused_computation.23 | convolution fusion | flops 1480720384 | bytes 11796480 | tf_op jit(solution)/shard_map/erf,edf->erd/dot_general | solution.py:50
  122.2 0.0 copy-start.2
  122.2 0.0 collective-permute-done
  122.2 4.3 %fusion.58 = f32[2,256,704]{1,2,0:T(8,128)} fusion(bf16[2,256,1024]{2,1,0:T(8,128)(2,1)} %bitcast.12, bf16[2,1024,704]{1,2,0:T(8,128)(2,1)} %collective-permute-done), kind=kOutput, calls=%fused_computation.74 | convolution fusion | flops 738197504 | bytes 5373952 | tf_op jit(solution)/shard_map/erd,edf->erf/dot_general | solution.py:44
  126.6 3.4 %collective-permute-done.2 = bf16[2,256,1024]{2,1,0:T(8,128)(2,1)} collective-permute-done((bf16[2,256,1024]{2,1,0:T(8,128)(2,1)}, bf16[2,256,1024]{2,1,0:T(8,128)(2,1)}, u32[]{:S(2)}, u32[]{:S(2)}) %collective-permute-start.2) | collective-permute-done | bytes 1048608 | tf_op jit(solution)/shard_map/ppermute | solution.py:114
  130.0 0.0 copy-done.2
  130.0 3.3 %fusion.60 = f32[2,256,704]{1,2,0:T(8,128)} fusion(bf16[2,256,1024]{2,1,0:T(8,128)(2,1)} %collective-permute-done.2, bf16[2,1024,704]{1,2,0:T(8,128)(2,1)S(1)} %copy-done.2), kind=kOutput, calls=%fused_computation.76 | convolution fusion | flops 738197504 | bytes 5373952 | tf_op jit(solution)/shard_map/erd,edf->erf/dot_general | solution.py:44
  133.2 4.2 %fusion.62 = f32[2,256,704]{1,2,0:T(8,128)} fusion(bf16[2,256,1024]{2,1,0:T(8,128)(2,1)} %collective-permute-done.2, bf16[2,1024,704]{1,2,0:T(8,128)(2,1)} %collective-permute-done), kind=kOutput, calls=%fused_computation.78 | convolution fusion | flops 738197504 | bytes 5373952 | tf_op jit(solution)/shard_map/erd,edf->erf/dot_general | solution.py:44
  137.5 14.1 %collective-permute-done.3 = bf16[2,256,1024]{2,1,0:T(8,128)(2,1)} collective-permute-done((bf16[2,256,1024]{2,1,0:T(8,128)(2,1)}, bf16[2,256,1024]{2,1,0:T(8,128)(2,1)}, u32[]{:S(2)}, u32[]{:S(2)}) %collective-permute-start.3) | collective-permute-done | bytes 1048608 | tf_op jit(solution)/shard_map/ppermute | solution.py:114
  151.5 3.3 %fusion.61 = f32[2,256,704]{1,2,0:T(8,128)} fusion(bf16[2,256,1024]{2,1,0:T(8,128)(2,1)} %collective-permute-done.3, bf16[2,1024,704]{1,2,0:T(8,128)(2,1)S(1)} %copy-done.2), kind=kOutput, calls=%fused_computation.77 | convolution fusion | flops 738197504 | bytes 5373952 | tf_op jit(solution)/shard_map/erd,edf->erf/dot_general | solution.py:45
  154.8 4.2 %fusion.63 = f32[2,256,704]{1,2,0:T(8,128)} fusion(bf16[2,256,1024]{2,1,0:T(8,128)(2,1)} %collective-permute-done.3, bf16[2,1024,704]{1,2,0:T(8,128)(2,1)} %collective-permute-done), kind=kOutput, calls=%fused_computation.79 | convolution fusion | flops 738197504 | bytes 5373952 | tf_op jit(solution)/shard_map/erd,edf->erf/dot_general | solution.py:45
  159.0 0.0 collective-permute-done.4
  159.0 7.4 %fusion.14 = f32[2,256,1024]{2,1,0:T(8,128)} fusion(bf16[2,1024,704]{1,2,0:T(8,128)(2,1)} %param.23, f32[2,256,704]{1,2,0:T(8,128)} %fusion.60, f32[2,256,704]{1,2,0:T(8,128)} %fusion.61, bf16[2,256,1024]{2,1,0:T(8,128)(2,1)} %collective-permute-done.4, bf16[2,1024,704]{1,2,0:T(8,128)(2,1)} %param.24), kind=kOutput, calls=%fused_computation.32 | convolution fusion | flops 1480720384 | bytes 11796480 | tf_op jit(solution)/shard_map/erf,edf->erd/dot_general | solution.py:50
  166.4 0.0 collective-permute-done.1
  166.4 7.8 %add_convert_fusion.1 = bf16[2,256,1024]{2,1,0:T(8,128)(2,1)} fusion(f32[2,256,1024]{2,1,0:T(8,128)} %fusion.14, bf16[2,1024,704]{1,2,0:T(8,128)(2,1)} %collective-permute-done, f32[2,256,704]{1,2,0:T(8,128)} %fusion.62, f32[2,256,704]{1,2,0:T(8,128)} %fusion.63, bf16[2,256,1024]{2,1,0:T(8,128)(2,1)} %collective-permute-done.4, ...), kind=kOutput, calls=%fused_computation.2 | convolution fusion | flops 1481768960 | bytes 12845056 | tf_op jit(solution)/shard_map/erf,edf->erd/dot_general | solution.py:50
  174.2 1.5 collective-permute-start.5
  175.7 4.2 %fusion.59 = f32[2,256,704]{1,2,0:T(8,128)} fusion(bf16[2,256,1024]{2,1,0:T(8,128)(2,1)} %bitcast.17, bf16[2,1024,704]{1,2,0:T(8,128)(2,1)} %collective-permute-done), kind=kOutput, calls=%fused_computation.75 | convolution fusion | flops 738197504 | bytes 5373952 | tf_op jit(solution)/shard_map/erd,edf->erf/dot_general | solution.py:45
  179.9 7.4 %fusion.13 = f32[2,256,1024]{2,1,0:T(8,128)} fusion(bf16[2,1024,704]{1,2,0:T(8,128)(2,1)} %collective-permute-done, f32[2,256,704]{1,2,0:T(8,128)} %fusion.58, f32[2,256,704]{1,2,0:T(8,128)} %fusion.59, bf16[2,256,1024]{2,1,0:T(8,128)(2,1)} %bitcast.22, bf16[2,1024,704]{1,2,0:T(8,128)(2,1)} %collective-permute-done.1), kind=kOutput, calls=%fused_computation.31 | convolution fusion | flops 1480720384 | bytes 11796480 | tf_op jit(solution)/shard_map/erf,edf->erd/dot_general | solution.py:50
  187.3 11.5 %collective-permute-done.5 = bf16[2,256,1024]{2,1,0:T(8,128)(2,1)} collective-permute-done((bf16[2,256,1024]{2,1,0:T(8,128)(2,1)}, bf16[2,256,1024]{2,1,0:T(8,128)(2,1)}, u32[]{:S(2)}, u32[]{:S(2)}) %collective-permute-start.5) | collective-permute-done | bytes 1048608 | tf_op jit(solution)/shard_map/ppermute | solution.py:119
  198.8 3.1 %add_convert_fusion = bf16[2,256,1024]{2,1,0:T(8,128)(2,1)S(1)} fusion(bf16[2,256,1024]{2,1,0:T(8,128)(2,1)} %collective-permute-done.5, f32[2,256,1024]{2,1,0:T(8,128)} %fusion.6, f32[2,256,1024]{2,1,0:T(8,128)} %fusion.13), kind=kLoop, calls=%fused_computation.1 | loop fusion | flops 2097152 | bytes 6291456 | tf_op jit(solution)/shard_map/convert_element_type | solution.py:122
  202.0 1.1 copy.45
  203.0 29.5 %all_to_all.69 = bf16[2,256,1024]{2,0,1:T(2,128)(2,1)S(1)} all-to-all(bf16[2,256,1024]{2,0,1:T(2,128)(2,1)S(1)} %copy.45), channel_id=1, replica_groups=mesh['expert'=8,'dp'=4] {'expert'}, dimensions={1} | all-to-all | bytes 2097152 | tf_op jit(solution)/shard_map/all_to_all | solution.py:121
  232.5 0.3 copy.46
  232.8 0.1 copy.47
  232.9 1.3 fusion.5
  (3 shorter events, 0.0 us)
Async XLA Ops:
  0.0 8.5 %copy-start = (bf16[1024,1024]{1,0:T(8,128)(2,1)S(1)}, bf16[1024,1024]{1,0:T(8,128)(2,1)}, u32[]{:S(2)}) copy-start(bf16[1024,1024]{1,0:T(8,128)(2,1)} %param.25) | copy-start | bytes 6291460
  8.5 0.8 copy-start.5
  8.5 0.8 copy-start.6
  8.5 0.8 copy-start.4
  9.4 10.0 %copy-start.3 = (f32[1024]{0:T(1024)S(1)}, f32[1024]{0:T(1024)}, u32[]{:S(2)}) copy-start(f32[1024]{0:T(1024)} %param.22) | copy-start | bytes 12292
  10.9 33.2 %all-to-all-start.2 = ((bf16[16,32,1024]{2,1,0:T(8,128)(2,1)}), bf16[16,32,1024]{2,1,0:T(8,128)(2,1)}, u32[]{:S(2)}, u32[]{:S(2)}) async-start(bf16[16,32,1024]{2,1,0:T(8,128)(2,1)} %bitcast.78), calls=%async_computation.2 | async-start | bytes 2097152 | tf_op jit(solution)/shard_map/all_to_all | solution.py:93
  44.0 29.8 %all-to-all-start = ((bf16[16,32,1024]{2,1,0:T(8,128)(2,1)}), bf16[16,32,1024]{2,1,0:T(8,128)(2,1)}, u32[]{:S(2)}, u32[]{:S(2)}) async-start(bf16[16,32,1024]{2,1,0:T(8,128)(2,1)} %bitcast.82), calls=%async_computation | async-start | bytes 2097152 | tf_op jit(solution)/shard_map/all_to_all | solution.py:93
  73.8 29.7 %all-to-all-start.1 = ((bf16[16,32,1024]{2,1,0:T(8,128)(2,1)}), bf16[16,32,1024]{2,1,0:T(8,128)(2,1)}, u32[]{:S(2)}, u32[]{:S(2)}) async-start(bf16[16,32,1024]{2,1,0:T(8,128)(2,1)} %bitcast.81), calls=%async_computation.1 | async-start | bytes 2097152 | tf_op jit(solution)/shard_map/all_to_all | solution.py:93
  78.3 44.0 %collective-permute-start = (bf16[2,1024,704]{1,2,0:T(8,128)(2,1)}, bf16[2,1024,704]{1,2,0:T(8,128)(2,1)}, u32[]{:S(2)}, u32[]{:S(2)}) collective-permute-start(bf16[2,1024,704]{1,2,0:T(8,128)(2,1)} %param.23), channel_id=1, source_target_pairs={{0,1},{1,0},{2,3},{3,2},{4,5},{5,4},{6,7},{7,6},{8,9},{9,8},{10,11... | collective-permute-start | bytes 8650760 | tf_op jit(solution)/shard_map/ppermute | solution.py:79
  78.4 88.1 %collective-permute-start.1 = (bf16[2,1024,704]{1,2,0:T(8,128)(2,1)}, bf16[2,1024,704]{1,2,0:T(8,128)(2,1)}, u32[]{:S(2)}, u32[]{:S(2)}) collective-permute-start(bf16[2,1024,704]{1,2,0:T(8,128)(2,1)} %param.24), channel_id=1, source_target_pairs={{0,1},{1,0},{2,3},{3,2},{4,5},{5,4},{6,7},{7,6},{8,9},{9,8},{10,11... | collective-permute-start | bytes 8650760 | tf_op jit(solution)/shard_map/ppermute | solution.py:79
  81.1 77.9 %collective-permute-start.4 = (bf16[2,256,1024]{2,1,0:T(8,128)(2,1)}, bf16[2,256,1024]{2,1,0:T(8,128)(2,1)}, u32[]{:S(2)}, u32[]{:S(2)}) collective-permute-start(bf16[2,256,1024]{2,1,0:T(8,128)(2,1)} %bitcast.22), channel_id=1, source_target_pairs={{0,2},{1,3},{2,0},{3,1},{4,6},{5,7},{6,4},{7,5},{8,10},{9,11},{10,... | collective-permute-start | bytes 3145736 | tf_op jit(solution)/shard_map/ppermute | solution.py:114
  85.0 45.0 %collective-permute-start.2 = (bf16[2,256,1024]{2,1,0:T(8,128)(2,1)}, bf16[2,256,1024]{2,1,0:T(8,128)(2,1)}, u32[]{:S(2)}, u32[]{:S(2)}) collective-permute-start(bf16[2,256,1024]{2,1,0:T(8,128)(2,1)} %bitcast.12), channel_id=1, source_target_pairs={{0,2},{1,3},{2,0},{3,1},{4,6},{5,7},{6,4},{7,5},{8,10},{9,11},{10,... | collective-permute-start | bytes 3145736 | tf_op jit(solution)/shard_map/ppermute | solution.py:114
  105.8 5.8 %copy-start.1 = (bf16[2,1024,704]{1,2,0:T(8,128)(2,1)S(1)}, bf16[2,1024,704]{1,2,0:T(8,128)(2,1)}, u32[]{:S(2)}) copy-start(bf16[2,1024,704]{1,2,0:T(8,128)(2,1)} %param.23) | copy-start | bytes 8650756
  105.8 45.7 %collective-permute-start.3 = (bf16[2,256,1024]{2,1,0:T(8,128)(2,1)}, bf16[2,256,1024]{2,1,0:T(8,128)(2,1)}, u32[]{:S(2)}, u32[]{:S(2)}) collective-permute-start(bf16[2,256,1024]{2,1,0:T(8,128)(2,1)} %bitcast.17), channel_id=1, source_target_pairs={{0,2},{1,3},{2,0},{3,1},{4,6},{5,7},{6,4},{7,5},{8,10},{9,11},{10,... | collective-permute-start | bytes 3145736 | tf_op jit(solution)/shard_map/ppermute | solution.py:114
  122.2 7.7 %copy-start.2 = (bf16[2,1024,704]{1,2,0:T(8,128)(2,1)S(1)}, bf16[2,1024,704]{1,2,0:T(8,128)(2,1)}, u32[]{:S(2)}) copy-start(bf16[2,1024,704]{1,2,0:T(8,128)(2,1)} %param.23) | copy-start | bytes 8650756
  174.2 24.6 %collective-permute-start.5 = (bf16[2,256,1024]{2,1,0:T(8,128)(2,1)}, bf16[2,256,1024]{2,1,0:T(8,128)(2,1)}, u32[]{:S(2)}, u32[]{:S(2)}) collective-permute-start(bf16[2,256,1024]{2,1,0:T(8,128)(2,1)} %add_convert_fusion.1), channel_id=1, source_target_pairs={{2,0},{3,1},{0,2},{1,3},{6,4},{7,5},{4,6},{5,7},{10,8},{11,9},{8,1... | collective-permute-start | bytes 3145736 | tf_op jit(solution)/shard_map/ppermute | solution.py:119

commit v2 on v0

--- a/solution.py
+++ b/solution.py
@@ -1,8 +1,11 @@
+import functools
 import math
 
 import jax
 import jax.numpy as jnp
 from jax import lax
+from jax.experimental import pallas as pl
+from jax.experimental.pallas import tpu as pltpu
 from jax.sharding import PartitionSpec as P
 
 HEADS = 16
@@ -48,6 +51,304 @@
     )
     act_mult = (rescale(pre_act, base_act) * hidden_mult).astype(jnp.bfloat16)
     return jnp.einsum("erf,edf->erd", act_mult, part_in, preferred_element_type=jnp.float32)
+
+
+def expert_kernel(
+    n_peers,
+    n_dp,
+    send_in,
+    send_base,
+    send_mult,
+    w_in,
+    w_out,
+    back,
+    all_in,
+    all_out,
+    near_rows,
+    far_rows,
+    ratio,
+    near_sum,
+    far_sum,
+    far_got,
+    slot_sum,
+    weight_sem,
+    swap_send,
+    swap_recv,
+    row_send,
+    row_recv,
+    hop_send,
+    hop_recv,
+    part_send,
+    part_recv,
+    back_send,
+    back_recv,
+):
+    sends = (send_in, send_base, send_mult)
+    n_local = w_in.shape[0]
+    cap = send_in.shape[1]
+    rows = n_peers * cap
+    me = lax.axis_index("expert")
+    dp = lax.axis_index("dp")
+    pair = dp + 1 - 2 * lax.rem(dp, 2)
+    across = lax.rem(dp + 2, n_dp)
+    mesh_id = pl.DeviceIdType.MESH
+
+    def peer_at(off):
+        return lax.rem(me + off, n_peers)
+
+    def source_at(off):
+        return lax.rem(me + n_peers - off, n_peers)
+
+    barrier = pltpu.get_barrier_semaphore()
+    for off in range(1, n_peers):
+        pl.semaphore_signal(barrier, inc=1, device_id={"expert": peer_at(off)}, device_id_type=mesh_id)
+    for other in (pair, across):
+        pl.semaphore_signal(barrier, inc=1, device_id={"dp": other}, device_id_type=mesh_id)
+    pl.semaphore_wait(barrier, n_peers + 1)
+
+    def row_block(buf, a, l, src):
+        return buf.at[a, l, pl.ds(pl.multiple_of(src * cap, cap), cap), :]
+
+    def row_copy(a, l, off):
+        peer = peer_at(off)
+        return pltpu.make_async_remote_copy(
+            src_ref=sends[a].at[peer * n_local + l],
+            dst_ref=row_block(near_rows, a, l, me),
+            send_sem=row_send.at[a, l, off],
+            recv_sem=row_recv.at[a, l, off],
+            device_id={"expert": peer},
+            device_id_type=mesh_id,
+        )
+
+    def own_copy(a, l):
+        return pltpu.make_async_copy(
+            sends[a].at[me * n_local + l], row_block(near_rows, a, l, me), row_recv.at[a, l, 0]
+        )
+
+    def send_rows(a, l):
+        for off in range(1, n_peers):
+            row_copy(a, l, off).start()
+        own_copy(a, l).start()
+
+    def hop_copy(a, l, off):
+        src = source_at(off)
+        return pltpu.make_async_remote_copy(
+            src_ref=row_block(near_rows, a, l, src),
+            dst_ref=row_block(far_rows, a, l, src),
+            send_sem=hop_send.at[a, l, off],
+            recv_sem=hop_recv.at[a, l, off],
+            device_id={"dp": across},
+            device_id_type=mesh_id,
+        )
+
+    def relay(a, l):
+        own_copy(a, l).wait()
+        hop_copy(a, l, 0).start()
+        for off in range(1, n_peers):
+            row_copy(a, l, off).wait_recv()
+            hop_copy(a, l, off).start()
+
+    def wait_far(a, l):
+        for off in range(n_peers):
+            hop_copy(a, l, off).wait_recv()
+
+    own_weights = []
+    for at, (ref, held) in enumerate(((w_in, all_in), (w_out, all_out))):
+        copy = pltpu.make_async_copy(ref, held.at[0], weight_sem.at[at])
+        copy.start()
+        own_weights.append(copy)
+    swaps = []
+    for l in range(n_local):
+        for a in range(3):
+            send_rows(a, l)
+        if l == 0:
+            for at, (ref, held) in enumerate(((w_in, all_in), (w_out, all_out))):
+                swap = pltpu.make_async_remote_copy(
+                    src_ref=ref,
+                    dst_ref=held.at[1],
+                    send_sem=swap_send.at[at],
+                    recv_sem=swap_recv.at[at],
+                    device_id={"dp": pair},
+                    device_id_type=mesh_id,
+                )
+                swap.start()
+                swaps.append(swap)
+
+    def ratio_of(buf, half, l):
+        @pl.loop(0, 2)
+        def _(shard):
+            weight = all_in[shard, l]
+            pre = jnp.dot(buf[0, l], weight, preferred_element_type=jnp.float32)
+            base = jnp.dot(buf[1, l], weight, preferred_element_type=jnp.float32)
+            ratio[half, shard] = rescale(pre, base)
+
+    def sum_of(buf, half, l, total):
+        @pl.loop(0, 2)
+        def _(shard):
+            hidden = jnp.dot(buf[2, l], all_out[shard, l], preferred_element_type=jnp.float32)
+            act = (ratio[half, shard] * hidden).astype(jnp.bfloat16)
+            part = lax.dot_general(
+                act, all_in[shard, l], (((1,), (1,)), ((), ())), preferred_element_type=jnp.float32
+            )
+
+            @pl.when(shard == 0)
+            def _():
+                total[...] = part
+
+            @pl.when(shard != 0)
+            def _():
+                total[...] += part
+
+    def part_copy(l):
+        return pltpu.make_async_remote_copy(
+            src_ref=far_sum.at[l],
+            dst_ref=far_got.at[l],
+            send_sem=part_send.at[l],
+            recv_sem=part_recv.at[l],
+            device_id={"dp": across},
+            device_id_type=mesh_id,
+        )
+
+    def back_copy(l, off):
+        peer = peer_at(off)
+        return pltpu.make_async_remote_copy(
+            src_ref=slot_sum.at[l, pl.ds(pl.multiple_of(peer * cap, cap), cap), :],
+            dst_ref=back.at[me * n_local + l],
+            send_sem=back_send.at[l, off],
+            recv_sem=back_recv.at[l, off],
+            device_id={"expert": peer},
+            device_id_type=mesh_id,
+        )
+
+    def own_back(l):
+        return pltpu.make_async_copy(
+            slot_sum.at[l, pl.ds(pl.multiple_of(me * cap, cap), cap), :],
+            back.at[me * n_local + l],
+            back_recv.at[l, 0],
+        )
+
+    def send_back(l):
+        part_copy(l).wait_recv()
+        slot_sum[l] = (near_sum[l] + far_got[l].astype(jnp.float32)).astype(jnp.bfloat16)
+        for off in range(1, n_peers):
+            back_copy(l, off).start()
+        own_back(l).start()
+
+    def far_part(l):
+        wait_far(0, l)
+        wait_far(1, l)
+        ratio_of(far_rows, 1, l)
+        wait_far(2, l)
+        sum_of(far_rows, 1, l, near_sum.at[n_local])
+        far_sum[l] = near_sum[n_local].astype(jnp.bfloat16)
+        part_copy(l).start()
+
+    relay(0, 0)
+    relay(1, 0)
+    for copy in own_weights:
+        copy.wait()
+    for swap in swaps:
+        swap.wait_recv()
+    ratio_of(near_rows, 0, 0)
+    relay(2, 0)
+    for l in range(n_local):
+        sum_of(near_rows, 0, l, near_sum.at[l])
+        if l + 1 < n_local:
+            relay(0, l + 1)
+        far_part(l)
+        if l + 1 < n_local:
+            relay(1, l + 1)
+            ratio_of(near_rows, 0, l + 1)
+            send_back(l)
+            relay(2, l + 1)
+    send_back(n_local - 1)
+
+    for swap in swaps:
+        swap.wait_send()
+    for l in range(n_local):
+        for a in range(3):
+            for off in range(n_peers):
+                if off:
+                    row_copy(a, l, off).wait_send()
+                hop_copy(a, l, off).wait_send()
+        part_copy(l).wait_send()
+        own_back(l).wait()
+        for off in range(1, n_peers):
+            back_copy(l, off).wait()
+
+
+def expert_pass(sent, w_in, w_out_t, n_peers, n_dp):
+    n_slots, cap, width = sent[0].shape
+    n_local, _, part = w_in.shape
+    rows = n_peers * cap
+    bf16, f32 = jnp.bfloat16, jnp.float32
+    dma = pltpu.SemaphoreType.DMA
+    vmem = pl.BlockSpec(memory_space=pltpu.VMEM)
+    anyw = pl.BlockSpec(memory_space=pl.ANY)
+    return pl.pallas_call(
+        functools.partial(expert_kernel, n_peers, n_dp),
+        out_shape=jax.ShapeDtypeStruct((n_slots, cap, width), bf16),
+        in_specs=[vmem, vmem, vmem, anyw, anyw],
+        out_specs=vmem,
+        scratch_shapes=[
+            pltpu.VMEM((2, n_local, width, part), bf16),
+            pltpu.VMEM((2, n_local, width, part), bf16),
+            pltpu.VMEM((3, n_local, rows, width), bf16),
+            pltpu.VMEM((3, n_local, rows, width), bf16),
+            pltpu.VMEM((2, 2, rows, part), f32),
+            pltpu.VMEM((n_local + 1, rows, width), f32),
+            pltpu.VMEM((n_local, rows, width), bf16),
+            pltpu.VMEM((n_local, rows, width), bf16),
+            pltpu.VMEM((n_local, rows, width), bf16),
+            dma((2,)),
+            dma((2,)),
+            dma((2,)),
+            dma((3, n_local, n_peers)),
+            dma((3, n_local, n_peers)),
+            dma((3, n_local, n_peers)),
+            dma((3, n_local, n_peers)),
+            dma((n_local,)),
+            dma((n_local,)),
+            dma((n_local, n_peers)),
+            dma((n_local, n_peers)),
+        ],
+        compiler_params=pltpu.CompilerParams(
+            collective_id=0, has_side_effects=True, vmem_limit_bytes=60 * 1024 * 1024
+        ),
+        name="expert_pass",
+    )(*sent, w_in, w_out_t)
+
+
+def plain_pass(sent, w_in, w_out_t, n_peers, n_dp):
+    near = 2 if n_dp % 2 == 0 else 1
+    shards = [(w_in, w_out_t)]
+    if near == 2:
+        swap = [(i, i ^ 1) for i in range(n_dp)]
+        shards.append((lax.ppermute(w_in, "dp", swap), lax.ppermute(w_out_t, "dp", swap)))
+    own_rows = tuple(
+        lax.all_to_all(a, "expert", split_axis=0, concat_axis=1, tiled=True) for a in sent
+    )
+
+    def partial_sum(rows):
+        total = expert_terms(*rows, *shards[0])
+        for part in shards[1:]:
+            total = total + expert_terms(*rows, *part)
+        return total
+
+    far = n_dp // near
+    far_rows = []
+    for hop in range(1, far):
+        ahead = [(i, (i + hop * near) % n_dp) for i in range(n_dp)]
+        far_rows.append(tuple(lax.ppermute(a, "dp", ahead) for a in own_rows))
+    slot_mult = partial_sum(own_rows)
+    for hop in range(1, far):
+        back = [((i + hop * near) % n_dp, i) for i in range(n_dp)]
+        far_part = partial_sum(far_rows[hop - 1]).astype(jnp.bfloat16)
+        slot_mult = slot_mult + lax.ppermute(far_part, "dp", back).astype(jnp.float32)
+
+    return lax.all_to_all(
+        slot_mult.astype(jnp.bfloat16), "expert", split_axis=1, concat_axis=0, tiled=True
+    )
 
 
 def body(
@@ -69,7 +370,9 @@
     feature_width = enc_state.shape[3]
     local_experts = w_in.shape[0]
     n_experts = local_experts * lax.axis_size("expert")
+    n_dp = lax.axis_size("dp")
     capacity = max(2, 2 * enc_len // n_experts)
+
     tokens = enc_state[0, 0].astype(jnp.float32)
     row_scale = norm_gain * lax.rsqrt(jnp.mean(tokens * tokens, axis=-1, keepdims=True) + 1e-06)
     inputs = (tokens * row_scale).astype(jnp.bfloat16)
@@ -87,21 +390,10 @@
         dec_queries[0, 0], enc_keys[0, 0], out_mult[0, 0], doc_lengths[0, 0], w_value
     )
     scaled_mult = (gate_prob[0, 0][:, None] * layer_mult).astype(jnp.bfloat16)
-    sent_in, sent_base, sent_mult = (
-        lax.all_to_all(dispatch(inputs), "expert", split_axis=0, concat_axis=1, tiled=True),
-        lax.all_to_all(dispatch(base_inputs), "expert", split_axis=0, concat_axis=1, tiled=True),
-        lax.all_to_all(dispatch(scaled_mult), "expert", split_axis=0, concat_axis=1, tiled=True),
-    )
-    slot_mult = expert_terms(
-        sent_in,
-        sent_base,
-        sent_mult,
-        lax.all_gather(w_in, "dp", axis=2, tiled=True),
-        lax.all_gather(w_out_t, "dp", axis=2, tiled=True),
-    )
-    returned = lax.all_to_all(
-        slot_mult.astype(jnp.bfloat16), "expert", split_axis=1, concat_axis=0, tiled=True
-    )
+    sent = (dispatch(inputs), dispatch(base_inputs), dispatch(scaled_mult))
+    n_peers = lax.axis_size("expert")
+    fits = n_dp == 4 and capacity % 16 == 0
+    returned = (expert_pass if fits else plain_pass)(sent, w_in, w_out_t, n_peers, n_dp)
     per_token = lax.dot_general(
         onehot,
         returned.reshape(n_experts * capacity, feature_width),

time: 231 us -> 166 us (0.72)
  the two profiles are of different devices: /device:TPU:0 before, /device:TPU:30 now
where the time goes in v2:
time: 166 us; the launch traced here: 165 us
  Pallas kernels  135 us (81%)
  matrix products  14.2 us (9%)
  local copies, waits for them, and re-layouts  13.4 us (8%)
  other arithmetic  2.01 us (1%)
    pallas_call x1, Pallas kernels, expert_pass(): pl.pallas_call(functools.partial(expert_kernel, n_peers, n_dp), out_shape...  135 us
    unnamed x13, local copies, waits for them, and re-layouts  13.4 us
    dot_general x3, matrix products, dispatch(): jnp.dot(onehot, values, preferred_element_type=jnp.float32)  5.74 us

profile of v2, /device:TPU:30, one launch (start us, length us, event | category | flops | bytes accessed | tf_op | source)
XLA Modules:
  0.0 165.0 jit_solution(2317239327522663563)
XLA Ops:
  0.0 0.0 copy-start
  0.0 0.0 copy-start.2
  0.8 0.7 multiply_add_fusion
  1.5 0.0 copy-start.1
  1.5 1.3 fusion.5
  2.8 1.8 %copy.19 = bf16[1,1,128,1024]{2,3,1,0:T(8,128)(2,1)} copy(bf16[1,1,128,1024]{3,2,1,0:T(8,128)(2,1)} %param.16) | data formatting | bytes 524288 | tf_op args[3]
  4.6 1.1 copy.21
  5.8 1.2 copy.20
  7.0 0.0 copy-done.2
  7.0 2.6 %convolution_convert_fusion.1 = bf16[512,1024]{1,0:T(8,128)(2,1)} fusion(bf16[1,1,256,1024]{3,2,1,0:T(8,128)(2,1)} %param.14, f32[256]{0:T(256)S(1)} %add_rsqrt_fusion, f32[1024]{0:T(1024)S(1)} %copy-done.2, s32[256]{0:T(256)S(1)} %bitcast.43), kind=kOutput, calls=%fused_computation.9 | convolution fusion | flops 270139392 | bytes 1579008 | tf_op jit(solution)/shard_map/dot_general | solution.py:386
  9.6 0.0 copy-done.1
  9.6 1.6 convolution_convert_fusion.2
  11.2 3.0 %fusion.28 = (f32[16,128]{1,0:T(8,128)S(1)}, f32[16,128,256]{2,1,0:T(8,128)}) fusion(pred[256]{0:T(512)(128)(4,1)S(1)} %iota_compare_fusion.5, bf16[128,16,64]{0,2,1:T(8,128)(2,1)} %bitcast.42, bf16[256,16,64]{0,2,1:T(8,128)(2,1)S(1)} %bitcast.40), kind=kOutput, calls=%fused_computation.41 | convolution fusion | flops 69206272 | bytes 2892032 | tf_op jit(solution)/shard_map/sub | solution.py:33
  14.2 2.1 %convolution_convert_fusion.3 = bf16[16,256,64]{1,2,0:T(8,128)(2,1)S(1)} fusion(bf16[128,16,64]{0,2,1:T(8,128)(2,1)S(1)} %bitcast.41, f32[16,128,256]{2,1,0:T(8,128)} %get-tuple-element.6, f32[16,128]{1,0:T(8,128)S(1)} %get-tuple-element.5), kind=kOutput, calls=%fused_computation.13 | convolution fusion | flops 68419584 | bytes 2891776 | tf_op jit(solution)/shard_map/hqk,qhd->khd/dot_general | solution.py:35
  16.3 0.0 copy-start.3
  16.3 0.0 copy-done
  16.3 0.8 fusion.29
  17.1 0.0 copy-done.3
  17.1 1.6 convolution_convert_fusion
  18.7 4.6 %copy.22.w_in = bf16[2,1024,704]{2,1,0:T(8,128)(2,1)} copy(bf16[2,1024,704]{1,2,0:T(8,128)(2,1)} %param.23) | data formatting | bytes 5767168 | tf_op args[10]
  23.3 4.6 %copy.23.w_out = bf16[2,1024,704]{2,1,0:T(8,128)(2,1)} copy(bf16[2,1024,704]{1,2,0:T(8,128)(2,1)} %param.24) | data formatting | bytes 5767168 | tf_op args[11]
  27.9 134.5 %expert_pass.1 = bf16[16,32,1024]{2,1,0:T(8,128)(2,1)} custom-call(bf16[16,32,1024]{2,1,0:T(8,128)(2,1)} %bitcast.38, bf16[16,32,1024]{2,1,0:T(8,128)(2,1)} %bitcast.37, bf16[16,32,1024]{2,1,0:T(8,128)(2,1)} %bitcast.35, bf16[2,1024,704]{2,1,0:T(8,128)(2,1)} %copy.22.w_in, bf16[2,1024,704]{2,1,0:T(8,128)(2,1)} %copy.23.w_out), custom_call_target="tpu_custom_call" | custom-call | tf_op jit(solution)/shard_map/expert_pass/pallas_call | solution.py:288
  162.5 2.5 %fusion.4 = bf16[1,1,256,1024]{3,2,1,0:T(8,128)(2,1)} fusion(f32[256,1024]{1,0:T(8,128)S(1)} %fusion.29, bf16[512,1024]{1,0:T(8,128)(2,1)} %bitcast.36, f32[256]{0:T(256)S(1)} %add_rsqrt_fusion, f32[1024]{0:T(1024)S(1)} %copy-done.2, s32[256]{0:T(256)S(1)} %bitcast.46), kind=kOutput, calls=%fused_computation.15 | convolution fusion | flops 269615104 | bytes 2627584 | tf_op jit(solution)/shard_map/dot_general | solution.py:397
  (2 shorter events, 0.0 us)
Async XLA Ops:
  0.0 16.3 %copy-start = (bf16[1024,1024]{1,0:T(8,128)(2,1)S(1)}, bf16[1024,1024]{1,0:T(8,128)(2,1)}, u32[]{:S(2)}) copy-start(bf16[1024,1024]{1,0:T(8,128)(2,1)} %param.25) | copy-start | bytes 6291460
  0.0 7.0 %copy-start.2 = (f32[1024]{0:T(1024)S(1)}, f32[1024]{0:T(1024)}, u32[]{:S(2)}) copy-start(f32[1024]{0:T(1024)} %param.22) | copy-start | bytes 12292
  1.5 8.1 %copy-start.1 = (bf16[1,1,256,1024]{3,2,1,0:T(8,128)(2,1)S(1)}, bf16[1,1,256,1024]{3,2,1,0:T(8,128)(2,1)}, u32[]{:S(2)}) copy-start(bf16[1,1,256,1024]{3,2,1,0:T(8,128)(2,1)} %param.13) | copy-start | bytes 1572868
  16.3 0.8 copy-start.3

commit v3 on v0

--- a/solution.py
+++ b/solution.py
@@ -1,8 +1,11 @@
+import functools
 import math
 
 import jax
 import jax.numpy as jnp
 from jax import lax
+from jax.experimental import pallas as pl
+from jax.experimental.pallas import tpu as pltpu
 from jax.sharding import PartitionSpec as P
 
 HEADS = 16
@@ -48,6 +51,454 @@
     )
     act_mult = (rescale(pre_act, base_act) * hidden_mult).astype(jnp.bfloat16)
     return jnp.einsum("erf,edf->erd", act_mult, part_in, preferred_element_type=jnp.float32)
+
+
+def times_t(left, right):
+    return lax.dot_general(left, right, (((1,), (1,)), ((), ())), preferred_element_type=jnp.float32)
+
+
+def whole_kernel(
+    n_peers,
+    n_dp,
+    cap,
+    chunk,
+    state,
+    base_state,
+    slot_row,
+    slot_col,
+    gate,
+    gain,
+    length,
+    keys_at,
+    queries_at,
+    mults_at,
+    value_at,
+    w_in,
+    w_out,
+    out,
+    keys,
+    queries,
+    mults,
+    value,
+    value_mult,
+    layer,
+    scale,
+    sends,
+    all_in,
+    all_out,
+    near_rows,
+    far_rows,
+    ratio,
+    act,
+    near_sum,
+    far_sum,
+    far_got,
+    slot_sum,
+    back,
+    load_sem,
+    weight_sem,
+    swap_send,
+    swap_recv,
+    row_send,
+    row_recv,
+    hop_send,
+    hop_recv,
+    part_send,
+    part_recv,
+    back_send,
+    back_recv,
+):
+    n_local = w_in.shape[0]
+    tokens, width = state.shape
+    rows = n_peers * cap
+    n_chunks = width // chunk
+    bf16, f32 = jnp.bfloat16, jnp.float32
+    me = lax.axis_index("expert")
+    dp = lax.axis_index("dp")
+    pair = dp + 1 - 2 * lax.rem(dp, 2)
+    across = lax.rem(dp + 2, n_dp)
+    mesh_id = pl.DeviceIdType.MESH
+
+    loads = []
+    for at, (ref, held) in enumerate(
+        ((queries_at, queries), (keys_at, keys), (mults_at, mults), (value_at, value))
+    ):
+        copy = pltpu.make_async_copy(ref, held, load_sem.at[at])
+        copy.start()
+        loads.append(copy)
+    own_weights = []
+    for at, (ref, held) in enumerate(((w_in, all_in), (w_out, all_out))):
+        copy = pltpu.make_async_copy(ref, held.at[0], weight_sem.at[at])
+        copy.start()
+        own_weights.append(copy)
+
+    def peer_at(step):
+        peer, bit = 0, 1
+        while bit < n_peers:
+            digit = lax.rem(me // bit, 2)
+            peer = peer + bit * (1 - digit if step & bit else digit)
+            bit *= 2
+        return peer
+
+    barrier = pltpu.get_barrier_semaphore()
+    for step in range(1, n_peers):
+        pl.semaphore_signal(barrier, inc=1, device_id={"expert": peer_at(step)}, device_id_type=mesh_id)
+    for other in (pair, across):
+        pl.semaphore_signal(barrier, inc=1, device_id={"dp": other}, device_id_type=mesh_id)
+
+    def place_rows(a, l, values):
+        at = lax.broadcasted_iota(jnp.int32, (rows, tokens), 0) + l * rows
+        onehot = jnp.where(at == slot_row[...], 1.0, 0.0).astype(bf16)
+        sends[a, l] = jnp.dot(onehot, values, preferred_element_type=f32).astype(bf16)
+
+    def block_of(src):
+        return pl.ds(pl.multiple_of(src * cap, cap), cap)
+
+    def row_copy(a, l, step):
+        peer = peer_at(step)
+        return pltpu.make_async_remote_copy(
+            src_ref=sends.at[a, l, block_of(peer), :],
+            dst_ref=near_rows.at[a, l, block_of(me), :],
+            send_sem=row_send.at[a, l, step],
+            recv_sem=row_recv.at[a, l, step],
+            device_id={"expert": peer},
+            device_id_type=mesh_id,
+        )
+
+    def own_copy(a, l):
+        return pltpu.make_async_copy(
+            sends.at[a, l, block_of(me), :], near_rows.at[a, l, block_of(me), :], row_recv.at[a, l, 0]
+        )
+
+    def send_rows(a, l):
+        own_copy(a, l).start()
+        for step in range(n_peers - 1, 0, -1):
+            row_copy(a, l, step).start()
+
+    def hop_copy(a, l, step):
+        src = block_of(peer_at(step))
+        return pltpu.make_async_remote_copy(
+            src_ref=near_rows.at[a, l, src, :],
+            dst_ref=far_rows.at[a, l, src, :],
+            send_sem=hop_send.at[a, l, step],
+            recv_sem=hop_recv.at[a, l, step],
+            device_id={"dp": across},
+            device_id_type=mesh_id,
+        )
+
+    def relay(a, l, steps):
+        for step in steps:
+            if step == 0:
+                own_copy(a, l).wait()
+            else:
+                row_copy(a, l, step).wait_recv()
+            hop_copy(a, l, step).start()
+
+    def wait_far(a, l):
+        for step in range(n_peers):
+            hop_copy(a, l, step).wait_recv()
+
+    close = range(0, 2)
+    distant = range(2, n_peers)
+
+    token_rows = state[...].astype(f32)
+    scale[...] = gain[...] * lax.rsqrt(
+        jnp.mean(token_rows * token_rows, axis=-1, keepdims=True) + 1e-06
+    )
+    inputs = (token_rows * scale[...]).astype(bf16)
+    place_rows(0, 0, inputs)
+    pl.semaphore_wait(barrier, n_peers + 1)
+    send_rows(0, 0)
+    base_inputs = (base_state[...].astype(f32) * scale[...]).astype(bf16)
+    place_rows(1, 0, base_inputs)
+    send_rows(1, 0)
+    for l in range(1, n_local):
+        place_rows(0, l, inputs)
+        send_rows(0, l)
+        place_rows(1, l, base_inputs)
+        send_rows(1, l)
+
+    swaps = []
+    for at, (ref, held) in enumerate(((w_in, all_in), (w_out, all_out))):
+        swap = pltpu.make_async_remote_copy(
+            src_ref=ref,
+            dst_ref=held.at[1],
+            send_sem=swap_send.at[at],
+            recv_sem=swap_recv.at[at],
+            device_id={"dp": pair},
+            device_id_type=mesh_id,
+        )
+        swap.start()
+        swaps.append(swap)
+
+    for l in range(n_local):
+        for a in range(2):
+            relay(a, l, close)
+
+    for copy in loads:
+        copy.wait()
+
+    @pl.loop(0, width // (2 * HEAD_DIM))
+    def _(both):
+        cols = pl.ds(pl.multiple_of(both * 2 * HEAD_DIM, 2 * HEAD_DIM), 2 * HEAD_DIM)
+        query, key, mult = queries[:, cols], keys[:, cols], mults[:, cols]
+        first = lax.broadcasted_iota(jnp.int32, query.shape, 1) < HEAD_DIM
+        zero = jnp.zeros_like(query)
+        found = []
+        for head in range(2):
+            mine = jnp.where(first, query, zero) if head == 0 else jnp.where(first, zero, query)
+            scores = times_t(key, mine) * (1.0 / math.sqrt(HEAD_DIM))
+            at = lax.broadcasted_iota(jnp.int32, scores.shape, 0)
+            scores = jnp.where(at < length[...], scores, -jnp.inf)
+            expo = jnp.exp(scores - jnp.max(scores, axis=0, keepdims=True))
+            attn = (expo / jnp.sum(expo, axis=0, keepdims=True)).astype(bf16)
+            found.append(jnp.dot(attn, mult, preferred_element_type=f32))
+        left = lax.broadcasted_iota(jnp.int32, found[0].shape, 1) < HEAD_DIM
+        value_mult[:, cols] = jnp.where(left, found[0], found[1]).astype(bf16)
+
+    def chunk_of(c):
+        return pl.ds(pl.multiple_of(c * chunk, chunk), chunk)
+
+    @pl.loop(0, n_chunks)
+    def _(c):
+        layer[:, chunk_of(c)] = times_t(value_mult[...], value[chunk_of(c), :])
+
+    scaled = (gate[...] * layer[...]).astype(bf16)
+    for l in range(n_local):
+        place_rows(2, l, scaled)
+        send_rows(2, l)
+    for l in range(n_local):
+        relay(2, l, close)
+
+    def ratio_of(buf, half, l):
+        @pl.loop(0, 2)
+        def _(shard):
+            weight = all_in[shard, l]
+            pre = times_t(buf[0, l], weight)
+            base = times_t(buf[1, l], weight)
+            ratio[half, l, shard] = rescale(pre, base)
+
+    def acts_of(buf, half, l):
+        @pl.loop(0, 2)
+        def _(shard):
+            hidden = times_t(buf[2, l], all_out[shard, l])
+            act[shard] = (ratio[half, l, shard] * hidden).astype(bf16)
+
+    def chunk_sum(l, c):
+        cols = chunk_of(c)
+        return jnp.dot(act[0], all_in[0, l, :, cols], preferred_element_type=f32) + jnp.dot(
+            act[1], all_in[1, l, :, cols], preferred_element_type=f32
+        )
+
+    def part_copy(l, c):
+        return pltpu.make_async_remote_copy(
+            src_ref=far_sum.at[l, :, chunk_of(c)],
+            dst_ref=far_got.at[l, :, chunk_of(c)],
+            send_sem=part_send.at[l, c],
+            recv_sem=part_recv.at[l, c],
+            device_id={"dp": across},
+            device_id_type=mesh_id,
+        )
+
+    def near_part(l):
+        acts_of(near_rows, 0, l)
+
+        @pl.loop(0, n_chunks)
+        def _(c):
+            near_sum[l, :, chunk_of(c)] = chunk_sum(l, c)
+
+    def far_part(l):
+        acts_of(far_rows, 1, l)
+
+        @pl.loop(0, n_chunks)
+        def _(c):
+            far_sum[l, :, chunk_of(c)] = chunk_sum(l, c).astype(bf16)
+            part_copy(l, c).start()
+
+    def back_copy(l, c, step):
+        peer = peer_at(step)
+        return pltpu.make_async_remote_copy(
+            src_ref=slot_sum.at[l, block_of(peer), chunk_of(c)],
+            dst_ref=back.at[l, block_of(me), chunk_of(c)],
+            send_sem=back_send.at[l, c, step],
+            recv_sem=back_recv.at[l, c, step],
+            device_id={"expert": peer},
+            device_id_type=mesh_id,
+        )
+
+    def own_back(l, c):
+        return pltpu.make_async_copy(
+            slot_sum.at[l, block_of(me), chunk_of(c)],
+            back.at[l, block_of(me), chunk_of(c)],
+            back_recv.at[l, c, 0],
+        )
+
+    def send_back(l):
+        @pl.loop(0, n_chunks)
+        def _(c):
+            part_copy(l, c).wait_recv()
+            cols = chunk_of(c)
+            slot_sum[l, :, cols] = (near_sum[l, :, cols] + far_got[l, :, cols].astype(f32)).astype(bf16)
+            for step in range(n_peers - 1, 0, -1):
+                back_copy(l, c, step).start()
+            own_back(l, c).start()
+
+    last = n_local - 1
+    for l in range(n_local):
+        relay(0, l, distant)
+        relay(1, l, distant)
+        if l == 0:
+            for copy in own_weights:
+                copy.wait()
+            for swap in swaps:
+                swap.wait_recv()
+        ratio_of(near_rows, 0, l)
+    for l in range(n_local):
+        wait_far(0, l)
+        wait_far(1, l)
+        if l == 0:
+            ratio_of(far_rows, 1, l)
+        relay(2, l, distant)
+        if l > 0:
+            ratio_of(far_rows, 1, l)
+        near_part(l)
+        if l > 0:
+            send_back(l - 1)
+        wait_far(2, l)
+        far_part(l)
+    send_back(last)
+
+    for l in range(n_local):
+        at = lax.broadcasted_iota(jnp.int32, (tokens, rows), 1) + l * rows
+        pick = jnp.where(at == slot_col[...], 1.0, 0.0).astype(bf16)
+        for c in range(n_chunks):
+            own_back(l, c).wait()
+            for step in range(1, n_peers):
+                back_copy(l, c, step).wait_recv()
+        term = jnp.dot(pick, back[l], preferred_element_type=f32)
+        if l == 0:
+            near_sum[0] = term
+        else:
+            near_sum[0] += term
+    out[...] = (layer[...] + scale[...] * near_sum[0]).astype(bf16)
+
+    for swap in swaps:
+        swap.wait_send()
+    for l in range(n_local):
+        for a in range(3):
+            for step in range(n_peers):
+                if step:
+                    row_copy(a, l, step).wait_send()
+                hop_copy(a, l, step).wait_send()
+        for c in range(n_chunks):
+            part_copy(l, c).wait_send()
+            for step in range(1, n_peers):
+                back_copy(l, c, step).wait_send()
+
+
+def whole_pass(
+    state, base_state, keys, queries, mults, length, slots, gate, gain, w_in, w_out_t, value, n_peers, n_dp, cap
+):
+    tokens, width = state.shape
+    n_local, _, part = w_in.shape
+    w_in, w_out_t = jnp.swapaxes(w_in, 1, 2), jnp.swapaxes(w_out_t, 1, 2)
+    rows = n_peers * cap
+    chunk = width // 4
+    n_chunks = width // chunk
+    bf16, f32 = jnp.bfloat16, jnp.float32
+    dma = pltpu.SemaphoreType.DMA
+    vmem = pl.BlockSpec(memory_space=pltpu.VMEM)
+    anyw = pl.BlockSpec(memory_space=pl.ANY)
+    wide = (n_local, rows, width)
+    return pl.pallas_call(
+        functools.partial(whole_kernel, n_peers, n_dp, cap, chunk),
+        out_shape=jax.ShapeDtypeStruct((tokens, width), bf16),
+        in_specs=[vmem] * 7 + [anyw] * 6,
+        out_specs=vmem,
+        scratch_shapes=[
+            pltpu.VMEM(keys.shape, bf16),
+            pltpu.VMEM(queries.shape, bf16),
+            pltpu.VMEM(mults.shape, bf16),
+            pltpu.VMEM(value.shape, bf16),
+            pltpu.VMEM((tokens, width), bf16),
+            pltpu.VMEM((tokens, width), f32),
+            pltpu.VMEM((tokens, width), f32),
+            pltpu.VMEM((3, *wide), bf16),
+            pltpu.VMEM((2, n_local, part, width), bf16),
+            pltpu.VMEM((2, n_local, part, width), bf16),
+            pltpu.VMEM((3, *wide), bf16),
+            pltpu.VMEM((3, *wide), bf16),
+            pltpu.VMEM((2, n_local, 2, rows, part), f32),
+            pltpu.VMEM((2, rows, part), bf16),
+            pltpu.VMEM(wide, f32),
+            pltpu.VMEM(wide, bf16),
+            pltpu.VMEM(wide, bf16),
+            pltpu.VMEM(wide, bf16),
+            pltpu.VMEM(wide, bf16),
+            dma((4,)),
+            dma((2,)),
+            dma((2,)),
+            dma((2,)),
+            dma((3, n_local, n_peers)),
+            dma((3, n_local, n_peers)),
+            dma((3, n_local, n_peers)),
+            dma((3, n_local, n_peers)),
+            dma((n_local, n_chunks)),
+            dma((n_local, n_chunks)),
+            dma((n_local, n_chunks, n_peers)),
+            dma((n_local, n_chunks, n_peers)),
+        ],
+        compiler_params=pltpu.CompilerParams(
+            collective_id=0, has_side_effects=True, vmem_limit_bytes=60 * 1024 * 1024
+        ),
+        name="whole_pass",
+    )(
+        state,
+        base_state,
+        slots[None, :],
+        slots[:, None],
+        gate[:, None],
+        gain[None, :],
+        length[None, None],
+        keys,
+        queries,
+        mults,
+        value,
+        w_in,
+        w_out_t,
+    )
+
+
+def plain_pass(sent, w_in, w_out_t, n_peers, n_dp):
+    near = 2 if n_dp % 2 == 0 else 1
+    shards = [(w_in, w_out_t)]
+    if near == 2:
+        swap = [(i, i ^ 1) for i in range(n_dp)]
+        shards.append((lax.ppermute(w_in, "dp", swap), lax.ppermute(w_out_t, "dp", swap)))
+    own_rows = tuple(
+        lax.all_to_all(a, "expert", split_axis=0, concat_axis=1, tiled=True) for a in sent
+    )
+
+    def partial_sum(rows):
+        total = expert_terms(*rows, *shards[0])
+        for part in shards[1:]:
+            total = total + expert_terms(*rows, *part)
+        return total
+
+    far = n_dp // near
+    far_rows = []
+    for hop in range(1, far):
+        ahead = [(i, (i + hop * near) % n_dp) for i in range(n_dp)]
+        far_rows.append(tuple(lax.ppermute(a, "dp", ahead) for a in own_rows))
+    slot_mult = partial_sum(own_rows)
+    for hop in range(1, far):
+        back = [((i + hop * near) % n_dp, i) for i in range(n_dp)]
+        far_part = partial_sum(far_rows[hop - 1]).astype(jnp.bfloat16)
+        slot_mult = slot_mult + lax.ppermute(far_part, "dp", back).astype(jnp.float32)
+
+    return lax.all_to_all(
+        slot_mult.astype(jnp.bfloat16), "expert", split_axis=1, concat_axis=0, tiled=True
+    )
 
 
 def body(
@@ -69,7 +520,35 @@
     feature_width = enc_state.shape[3]
     local_experts = w_in.shape[0]
     n_experts = local_experts * lax.axis_size("expert")
+    n_dp = lax.axis_size("dp")
     capacity = max(2, 2 * enc_len // n_experts)
+
+    n_peers = lax.axis_size("expert")
+    if n_dp == 4 and local_experts == 2 and capacity % 16 == 0 and n_peers & (n_peers - 1) == 0 and feature_width % 512 == 0:
+        expert = expert_ids[0, 0]
+        slots = (
+            lax.rem(expert, local_experts) * (n_peers * capacity)
+            + (expert // local_experts) * capacity
+            + slot_ids[0, 0]
+        )
+        return whole_pass(
+            enc_state[0, 0],
+            baseline[0, 0],
+            enc_keys[0, 0],
+            dec_queries[0, 0],
+            out_mult[0, 0],
+            doc_lengths[0, 0],
+            slots,
+            gate_prob[0, 0],
+            norm_gain,
+            w_in,
+            w_out_t,
+            w_value,
+            n_peers,
+            n_dp,
+            capacity,
+        )[None, None]
+
     tokens = enc_state[0, 0].astype(jnp.float32)
     row_scale = norm_gain * lax.rsqrt(jnp.mean(tokens * tokens, axis=-1, keepdims=True) + 1e-06)
     inputs = (tokens * row_scale).astype(jnp.bfloat16)
@@ -87,21 +566,8 @@
         dec_queries[0, 0], enc_keys[0, 0], out_mult[0, 0], doc_lengths[0, 0], w_value
     )
     scaled_mult = (gate_prob[0, 0][:, None] * layer_mult).astype(jnp.bfloat16)
-    sent_in, sent_base, sent_mult = (
-        lax.all_to_all(dispatch(inputs), "expert", split_axis=0, concat_axis=1, tiled=True),
-        lax.all_to_all(dispatch(base_inputs), "expert", split_axis=0, concat_axis=1, tiled=True),
-        lax.all_to_all(dispatch(scaled_mult), "expert", split_axis=0, concat_axis=1, tiled=True),
-    )
-    slot_mult = expert_terms(
-        sent_in,
-        sent_base,
-        sent_mult,
-        lax.all_gather(w_in, "dp", axis=2, tiled=True),
-        lax.all_gather(w_out_t, "dp", axis=2, tiled=True),
-    )
-    returned = lax.all_to_all(
-        slot_mult.astype(jnp.bfloat16), "expert", split_axis=1, concat_axis=0, tiled=True
-    )
+    sent = (dispatch(inputs), dispatch(base_inputs), dispatch(scaled_mult))
+    returned = plain_pass(sent, w_in, w_out_t, n_peers, n_dp)
     per_token = lax.dot_general(
         onehot,
         returned.reshape(n_experts * capacity, feature_width),

time: 231 us -> 134 us (0.58)
  Pallas kernels: 0 us -> 126 us
  waiting for transfers between devices: 96.8 us -> 0 us
  matrix products: 62.3 us -> 0 us
  blocking collectives: 31.4 us -> 0 us
  starting transfers between devices: 15.3 us -> 0 us
  between operations: 14.2 us -> 0.68 us
  local copies, waits for them, and re-layouts: 10.3 us -> 4.95 us
    pallas_call x0 -> x1, Pallas kernels: none -> 126 us  [whole_pass(): pl.pallas_call(functools.partial(whole_kernel, n_peers, n_dp, cap, chunk)...]
    dot_general x10 -> x0, matrix products: 59.1 us -> none  [the longest x1 15.6 us: expert_terms(): jnp.einsum('erd,edf->erf', rows_mult, part_out, preferred_element_type=jn...]
    all_to_all x3 -> x0, waiting for transfers between devices: 58.3 us -> none  [the longest x1 23.1 us: body(): lax.all_to_all(dispatch(base_inputs), 'expert', split_axis=0, concat_axis...]
    all_gather x2 -> x0, waiting for transfers between devices: 37.1 us -> none  [the longest x1 37.1 us: body(): lax.all_gather(w_out_t, 'dp', axis=2, tiled=True)]
    all_to_all x1 -> x0, blocking collectives: 31.4 us -> none  [body(): lax.all_to_all(slot_mult.astype(jnp.bfloat16), 'expert', split_axis=1, co...]
    all_to_all x3 -> x0, starting transfers between devices: 15.3 us -> none  [the longest x1 7.28 us: body(): lax.all_to_all(dispatch(base_inputs), 'expert', split_axis=0, concat_axis...]
    all_to_all x5 -> x0, local copies, waits for them, and re-layouts: 5.19 us -> none  [the longest x1 2.43 us: body(): lax.all_to_all(dispatch(inputs), 'expert', split_axis=0, concat_axis=1, t...]
    sub x1 -> x0, matrix products: 3.16 us -> none  [attend(): expo = jnp.exp(scores - top_score)]
  transfers between devices with their start and end apart: 5 -> 0, of which waited for: 4 -> 0; matrix products, arithmetic and copies ran while one was open for 20% -> 0% of each run, Pallas kernels for 0% -> 0%
where the time goes in v3:
time: 134 us; the launch traced here: 133 us
  Pallas kernels  126 us (94%)
  local copies, waits for them, and re-layouts  4.95 us (4%)
  other arithmetic  2 us (1%)
    pallas_call x1, Pallas kernels, whole_pass(): pl.pallas_call(functools.partial(whole_kernel, n_peers, n_dp, cap, chunk)...  126 us

profile of v3, /device:TPU:0, one launch (start us, length us, event | category | flops | bytes accessed | tf_op | source)
XLA Modules:
  0.0 133.4 jit_solution(6946623820646750237)
XLA Ops:
  0.7 1.2 bitcast_add_fusion.slot_row
  1.9 1.5 %copy.26.gate = f32[256,1]{1,0:T(8,128)} copy(f32[256,1]{0,1:T(1,128)} %bitcast.38) | data formatting | bytes 2048 | tf_op jit(solution)/shard_map/broadcast_in_dim;squeeze | solution.py:460
  3.4 0.8 copy.25
  4.2 0.8 copy.20
  5.0 0.8 fusion.2.slot_col
  5.7 125.8 %whole_pass.1 = bf16[256,1024]{1,0:T(8,128)(2,1)} custom-call(bf16[256,1024]{1,0:T(8,128)(2,1)} %bitcast.30, bf16[256,1024]{1,0:T(8,128)(2,1)} %bitcast.31, s32[1,256]{1,0:T(1,128)} %bitcast_add_fusion.slot_row, s32[256,1]{1,0:T(8,128)} %fusion.2.slot_col, f32[256,1]{1,0:T(8,128)} %copy.26.gate, f32[1,1024]{1,0:T(1,128)} %bitcast.35, ...), custom_call_target="tpu_custom_call" | custom-call | tf_op jit(solution)/shard_map/whole_pass/pallas_call | solution.py:413
  131.6 1.9 %copy.29 = bf16[1,1,256,1024]{3,2,1,0:T(8,128)(2,1)} copy(bf16[1,1,256,1024]{3,2,1,0:T(8,128)(2,1)} %bitcast.29) | data formatting | bytes 1048576

commit v4 on v3

--- a/solution.py
+++ b/solution.py
@@ -64,8 +64,8 @@
     chunk,
     state,
     base_state,
-    slot_row,
-    slot_col,
+    expert_row,
+    place_row,
     gate,
     gain,
     length,
@@ -146,9 +146,17 @@
     for other in (pair, across):
         pl.semaphore_signal(barrier, inc=1, device_id={"dp": other}, device_id_type=mesh_id)
 
+    expert = expert_row[...]
+    slot_row = (
+        lax.rem(expert, n_local) * rows + lax.div(expert, n_local) * cap + place_row[...]
+    )
+
+    def column(row):
+        return jnp.transpose(jnp.broadcast_to(row, (128, tokens)))[:, :1]
+
     def place_rows(a, l, values):
         at = lax.broadcasted_iota(jnp.int32, (rows, tokens), 0) + l * rows
-        onehot = jnp.where(at == slot_row[...], 1.0, 0.0).astype(bf16)
+        onehot = jnp.where(at == slot_row, 1.0, 0.0).astype(bf16)
         sends[a, l] = jnp.dot(onehot, values, preferred_element_type=f32).astype(bf16)
 
     def block_of(src):
@@ -238,8 +246,7 @@
     for copy in loads:
         copy.wait()
 
-    @pl.loop(0, width // (2 * HEAD_DIM))
-    def _(both):
+    def two_heads(both):
         cols = pl.ds(pl.multiple_of(both * 2 * HEAD_DIM, 2 * HEAD_DIM), 2 * HEAD_DIM)
         query, key, mult = queries[:, cols], keys[:, cols], mults[:, cols]
         first = lax.broadcasted_iota(jnp.int32, query.shape, 1) < HEAD_DIM
@@ -256,6 +263,13 @@
         left = lax.broadcasted_iota(jnp.int32, found[0].shape, 1) < HEAD_DIM
         value_mult[:, cols] = jnp.where(left, found[0], found[1]).astype(bf16)
 
+    pieces = width // (2 * HEAD_DIM)
+    bounds = [pieces * at // 4 for at in range(5)]
+    for at in range(4):
+        pl.loop(bounds[at], bounds[at + 1])(two_heads)
+        if at < 2:
+            relay(at, 0, distant)
+
     def chunk_of(c):
         return pl.ds(pl.multiple_of(c * chunk, chunk), chunk)
 
@@ -263,7 +277,7 @@
     def _(c):
         layer[:, chunk_of(c)] = times_t(value_mult[...], value[chunk_of(c), :])
 
-    scaled = (gate[...] * layer[...]).astype(bf16)
+    scaled = (column(gate[...]) * layer[...]).astype(bf16)
     for l in range(n_local):
         place_rows(2, l, scaled)
         send_rows(2, l)
@@ -345,8 +359,9 @@
 
     last = n_local - 1
     for l in range(n_local):
-        relay(0, l, distant)
-        relay(1, l, distant)
+        if l > 0:
+            relay(0, l, distant)
+            relay(1, l, distant)
         if l == 0:
             for copy in own_weights:
                 copy.wait()
@@ -368,9 +383,10 @@
         far_part(l)
     send_back(last)
 
+    slot_col = column(slot_row.astype(f32))
     for l in range(n_local):
         at = lax.broadcasted_iota(jnp.int32, (tokens, rows), 1) + l * rows
-        pick = jnp.where(at == slot_col[...], 1.0, 0.0).astype(bf16)
+        pick = jnp.where(at.astype(f32) == slot_col, 1.0, 0.0).astype(bf16)
         for c in range(n_chunks):
             own_back(l, c).wait()
             for step in range(1, n_peers):
@@ -397,7 +413,7 @@
 
 
 def whole_pass(
-    state, base_state, keys, queries, mults, length, slots, gate, gain, w_in, w_out_t, value, n_peers, n_dp, cap
+    state, base_state, keys, queries, mults, length, expert, place, gate, gain, w_in, w_out_t, value, n_peers, n_dp, cap
 ):
     tokens, width = state.shape
     n_local, _, part = w_in.shape
@@ -455,11 +471,11 @@
     )(
         state,
         base_state,
-        slots[None, :],
-        slots[:, None],
-        gate[:, None],
+        expert,
+        place,
+        gate,
         gain[None, :],
-        length[None, None],
+        length,
         keys,
         queries,
         mults,
@@ -525,21 +541,16 @@
 
     n_peers = lax.axis_size("expert")
     if n_dp == 4 and local_experts == 2 and capacity % 16 == 0 and n_peers & (n_peers - 1) == 0 and feature_width % 512 == 0:
-        expert = expert_ids[0, 0]
-        slots = (
-            lax.rem(expert, local_experts) * (n_peers * capacity)
-            + (expert // local_experts) * capacity
-            + slot_ids[0, 0]
-        )
         return whole_pass(
             enc_state[0, 0],
             baseline[0, 0],
             enc_keys[0, 0],
             dec_queries[0, 0],
             out_mult[0, 0],
-            doc_lengths[0, 0],
-            slots,
-            gate_prob[0, 0],
+            doc_lengths,
+            expert_ids[0],
+            slot_ids[0],
+            gate_prob[0],
             norm_gain,
             w_in,
             w_out_t,

time: 134 us -> 129 us (0.963)
  local copies, waits for them, and re-layouts: 4.95 us -> 1.87 us
  other arithmetic: 2 us -> 0 us
    add x2 -> x0, other arithmetic: 2 us -> none  [body(): lax.rem(expert, local_experts) * (n_peers * capacity)]
    squeeze x2 -> x0, local copies, waits for them, and re-layouts: 1.62 us -> none  [the longest x1 0.81 us: body(): expert = expert_ids[0, 0]]
    another operation x1 -> x0, local copies, waits for them, and re-layouts: 1.47 us -> none  [whole_pass(): gate[:, None]]
where the time goes in v4:
time: 129 us
  Pallas kernels  127 us (98%)
  local copies, waits for them, and re-layouts  1.87 us (1%)
    pallas_call x1, Pallas kernels, whole_pass(): pl.pallas_call(functools.partial(whole_kernel, n_peers, n_dp, cap, chunk)...  127 us

profile of v4, /device:TPU:0, one launch (start us, length us, event | category | flops | bytes accessed | tf_op | source)
XLA Modules:
  0.0 129.2 jit_solution(3692540756289901077)
XLA Ops:
  0.7 126.7 %whole_pass.1 = bf16[256,1024]{1,0:T(8,128)(2,1)} custom-call(bf16[256,1024]{1,0:T(8,128)(2,1)} %bitcast.15, bf16[256,1024]{1,0:T(8,128)(2,1)} %bitcast.16, s32[1,256]{1,0:T(1,128)} %bitcast.21, s32[1,256]{1,0:T(1,128)} %bitcast.22, f32[1,256]{1,0:T(1,128)} %bitcast.23, f32[1,1024]{1,0:T(1,128)} %bitcast.20, s32[1,1]{1,0:T(1,128)S(6)} %copy.15.length, ...), custom_call_target="tpu_custom_call" | custom-call | tf_op jit(solution)/shard_map/whole_pass/pallas_call | solution.py:429
  127.3 1.9 %copy.16 = bf16[1,1,256,1024]{3,2,1,0:T(8,128)(2,1)} copy(bf16[1,1,256,1024]{3,2,1,0:T(8,128)(2,1)} %bitcast.14) | data formatting | bytes 1048576

commit v5 on v4

--- a/solution.py
+++ b/solution.py
@@ -224,7 +224,6 @@
         place_rows(0, l, inputs)
         send_rows(0, l)
         place_rows(1, l, base_inputs)
-        send_rows(1, l)
 
     swaps = []
     for at, (ref, held) in enumerate(((w_in, all_in), (w_out, all_out))):
@@ -239,9 +238,10 @@
         swap.start()
         swaps.append(swap)
 
-    for l in range(n_local):
-        for a in range(2):
-            relay(a, l, close)
+    relay(0, 0, close)
+    relay(1, 0, close)
+    for l in range(1, n_local):
+        relay(0, l, close)
 
     for copy in loads:
         copy.wait()
@@ -267,8 +267,8 @@
     bounds = [pieces * at // 4 for at in range(5)]
     for at in range(4):
         pl.loop(bounds[at], bounds[at + 1])(two_heads)
-        if at < 2:
-            relay(at, 0, distant)
+        if at == 1:
+            relay(0, 0, distant)
 
     def chunk_of(c):
         return pl.ds(pl.multiple_of(c * chunk, chunk), chunk)
@@ -280,8 +280,12 @@
     scaled = (column(gate[...]) * layer[...]).astype(bf16)
     for l in range(n_local):
         place_rows(2, l, scaled)
+        if l > 0:
+            send_rows(1, l)
         send_rows(2, l)
     for l in range(n_local):
+        if l > 0:
+            relay(1, l, close)
         relay(2, l, close)
 
     def ratio_of(buf, half, l):
@@ -359,24 +363,22 @@
 
     last = n_local - 1
     for l in range(n_local):
-        if l > 0:
+        if l > 1:
             relay(0, l, distant)
-            relay(1, l, distant)
+        relay(1, l, distant)
         if l == 0:
             for copy in own_weights:
                 copy.wait()
             for swap in swaps:
                 swap.wait_recv()
         ratio_of(near_rows, 0, l)
-    for l in range(n_local):
+        if l == 0 and n_local > 1:
+            relay(0, 1, distant)
+        relay(2, l, distant)
+        near_part(l)
         wait_far(0, l)
         wait_far(1, l)
-        if l == 0:
-            ratio_of(far_rows, 1, l)
-        relay(2, l, distant)
-        if l > 0:
-            ratio_of(far_rows, 1, l)
-        near_part(l)
+        ratio_of(far_rows, 1, l)
         if l > 0:
             send_back(l - 1)
         wait_far(2, l)

time: 129 us -> 129 us (level)
  no operation moved by 1% of the time
where the time goes in v5:
time: 129 us; the launch traced here: 128 us
  Pallas kernels  126 us (98%)
  local copies, waits for them, and re-layouts  1.87 us (1%)
    pallas_call x1, Pallas kernels, whole_pass(): pl.pallas_call(functools.partial(whole_kernel, n_peers, n_dp, cap, chunk)...  126 us

profile of v5, /device:TPU:0, one launch (start us, length us, event | category | flops | bytes accessed | tf_op | source)
XLA Modules:
  0.0 128.5 jit_solution(10506066896986776579)
XLA Ops:
  0.7 125.9 %whole_pass.1 = bf16[256,1024]{1,0:T(8,128)(2,1)} custom-call(bf16[256,1024]{1,0:T(8,128)(2,1)} %bitcast.15, bf16[256,1024]{1,0:T(8,128)(2,1)} %bitcast.16, s32[1,256]{1,0:T(1,128)} %bitcast.21, s32[1,256]{1,0:T(1,128)} %bitcast.22, f32[1,256]{1,0:T(1,128)} %bitcast.23, f32[1,1024]{1,0:T(1,128)} %bitcast.20, s32[1,1]{1,0:T(1,128)S(6)} %copy.15.length, ...), custom_call_target="tpu_custom_call" | custom-call | tf_op jit(solution)/shard_map/whole_pass/pallas_call | solution.py:431
  126.6 1.9 %copy.16 = bf16[1,1,256,1024]{3,2,1,0:T(8,128)(2,1)} copy(bf16[1,1,256,1024]{3,2,1,0:T(8,128)(2,1)} %bitcast.14) | data formatting | bytes 1048576
